TPU v7x, 32 devices: a whole 2x2x4 slice. The times are simulated.
32 devices in a mesh: pt: 8 (over z, y), tm: 4 (over x, core).
Axes of the slice: x: 2, y: 2, z: 4, core: 2. Of those that a mesh axis runs over, the one named last changes fastest.
Arguments:
- signals: float32 [512, 32768], P('pt', 'tm'), may hold values from -6 to 6
- freq_bins: int32 [4], replicated, may hold values from 1 to 511
Outputs:
- cross_spectra: float32 [2, 4, 512, 512], P(None, None, 'pt', 'tm')
All inputs are finite; a program needn't handle non-finite values.
Results may differ from a plain program's by a relative error of at most 0.000064.
Values sent between devices are 32-bit elements; how exact they have to be, the bound alone decides.
No kernel may reach another device: no remote copies, remote signals or barrier semaphores. Data moves between devices by JAX's collectives and lax.ppermute only.
A program may use at most 64 MiB of HBM per device.

v0:
```python
import math

import jax
import jax.numpy as jnp
from jax import lax
from jax.sharding import PartitionSpec as P

SEGLEN = 1024


TWO_PI = 2.0 * math.pi


def shifted(value, axis, steps):
    count = lax.axis_size(axis)
    initial, last = (max(0, -steps), min(count, count - steps))
    return lax.ppermute(value, axis, [(source, source + steps) for source in range(initial, last)])


def dft_tables(freq_bins, seg_len):
    sample_index = jnp.arange(seg_len, dtype=jnp.int32)
    wrapped = sample_index[:, None] * freq_bins[None, :] % seg_len
    angles = wrapped.astype(jnp.float32) * (TWO_PI / seg_len)
    window = 0.5 - 0.5 * jnp.cos(sample_index.astype(jnp.float32) * (TWO_PI / seg_len))
    cosine = window[:, None] * jnp.cos(angles)
    sine_part = -window[:, None] * jnp.sin(angles)
    full_table = jnp.concatenate([cosine, sine_part], axis=1)
    half_len = seg_len // 2
    return jnp.concatenate([full_table[:half_len], full_table[half_len:]], axis=1)


def tile_products(left_side, right_side):
    stacked_right = jnp.concatenate([right_side[:, 0], right_side[:, 1]], axis=2)
    real_left = jnp.concatenate([left_side[:, 0], left_side[:, 1]], axis=2)
    imag_left = jnp.concatenate([left_side[:, 1], -left_side[:, 0]], axis=2)
    real_part = jnp.einsum(
        "fps,fqs->fpq", real_left, stacked_right, precision=lax.Precision.HIGHEST
    )
    imag_part = jnp.einsum(
        "fps,fqs->fpq", imag_left, stacked_right, precision=lax.Precision.HIGHEST
    )
    return jnp.stack([real_part, imag_part])


def body(signals, freq_bins):
    point_rows, sample_count = signals.shape
    half_len = SEGLEN // 2
    blocks_dev = sample_count // half_len
    bin_count = freq_bins.shape[0]
    columns = 2 * bin_count
    table = dft_tables(freq_bins, SEGLEN)
    blocks = signals.reshape(point_rows, blocks_dev, half_len)
    projected = jnp.einsum("pbn,nc->pbc", blocks, table, precision=lax.Precision.HIGHEST)
    incoming = shifted(signals[:, :half_len], "tm", -1)
    boundary = jnp.dot(
        incoming,
        table[:, columns:],
        precision=lax.Precision.HIGHEST,
        preferred_element_type=jnp.float32,
    )
    following = jnp.concatenate([projected[:, 1:, columns:], boundary[:, None, :]], axis=1)
    spectra = projected[:, :, :columns] + following
    is_last = lax.axis_index("tm") == lax.axis_size("tm") - 1
    segment_ids = jnp.arange(blocks_dev, dtype=jnp.int32)
    weight_mask = jnp.where(
        jnp.logical_and(is_last, segment_ids == blocks_dev - 1), 0.0, 1.0
    ).astype(jnp.float32)
    spectra = spectra * weight_mask[None, :, None]
    spectra_panel = spectra.reshape(point_rows, blocks_dev, 2, bin_count).transpose(3, 2, 0, 1)
    partial_tiles = tile_products(
        spectra_panel, lax.all_gather(spectra_panel, "pt", axis=2, tiled=True)
    )
    summed = lax.psum_scatter(partial_tiles, "tm", scatter_dimension=3, tiled=True)
    total_segments = blocks_dev * lax.axis_size("tm") - 1
    scale = 1.0 / (total_segments * 0.375 * SEGLEN)
    return summed * scale


def solution(mesh):
    in_specs = (P("pt", "tm"), P())
    out_specs = P(None, None, "pt", "tm")
    return jax.shard_map(body, mesh=mesh, in_specs=in_specs, out_specs=out_specs, check_vma=False)
```

profile of v0, /device:TPU:0, one launch (start us, length us, event | category | flops | bytes accessed | tf_op | source)
XLA Modules:
  0.0 97.8 jit_solution(1529557021851676892)
XLA Ops:
  6.5 0.0 reduce-scatter.2.cloned.1.call-start
  6.5 0.9 slice.33
  7.5 1.3 %collective-permute-start = (f32[64,512]{1,0:T(8,128)S(1)}, f32[64,512]{1,0:T(8,128)S(1)}, u32[]{:S(2)}, u32[]{:S(2)}) collective-permute-start(f32[64,512]{1,0:T(8,128)S(1)} %slice.33), channel_id=1, source_target_pairs={{1,0},{2,1},{3,2},{5,4},{6,5},{7,6},{9,8},{10,9},{11,10},{13,12},{... | collective-permute-start | bytes 393224 | tf_op jit(solution)/shard_map/ppermute | solution.py:17
  8.8 0.9 cosine_multiply_fusion
  9.7 4.2 %fusion.3 = f32[64,16,16]{0,2,1:T(8,128)S(1)} fusion(f32[8,16,8,512]{3,2,1,0:T(8,128)} %bitcast.33, f32[512,8]{0,1:T(8,128)S(1)} %get-tuple-element.10, f32[512,8]{0,1:T(8,128)S(1)} %get-tuple-element.9), kind=kOutput, calls=%fused_computation.5 | convolution fusion | flops 100671488 | bytes 2195456 | tf_op jit(solution)/shard_map/pbn,nc->pbc/dot_general | solution.py:53
  13.9 0.0 collective-permute-done
  13.9 0.2 convolution_bitcast_fusion.2
  14.1 0.1 fusion.6
  14.2 0.2 copy.7
  14.4 47.1 %all_gather.3 = f32[4,2,512,16]{3,0,1,2:T(4,128)S(1)} all-gather(f32[4,2,64,16]{3,0,1,2:T(4,128)S(1)} %copy.7), channel_id=1, replica_groups=mesh['pt'=8,'tm'=4] {'pt'}, dimensions={2}, use_global_device_ids=true | all-gather | bytes 294912 | tf_op jit(solution)/shard_map/all_gather | solution.py:71
  61.5 0.4 fusion.24
  61.9 0.3 copy.10
  62.2 0.3 copy.11
  62.5 0.6 convolution_bitcast_fusion.1
  63.2 0.6 convolution_bitcast_fusion
  63.8 1.0 %pad_maximum_fusion = f32[2,4,64,512]{3,2,1,0:T(8,128)} fusion(f32[1,4,64,512]{3,2,1,0:T(8,128)S(1)} %convolution_bitcast_fusion, f32[1,4,64,512]{3,2,1,0:T(8,128)S(1)} %convolution_bitcast_fusion.1), kind=kLoop, calls=%fused_computation.7 | loop fusion | flops 262144 | bytes 2097152 | tf_op jit(solution)/shard_map/stack | solution.py:42
  64.9 0.0 reduce-scatter.2.cloned.1.call-update
  64.9 24.3 %reduce-scatter.2.cloned.1.call-done = f32[2,4,64,128]{3,2,1,0:T(8,128)} async-done(((f32[2,4,64,512]{3,2,1,0:T(8,128)}), f32[2,4,64,128]{3,2,1,0:T(8,128)}) %reduce-scatter.2.cloned.1.call-update) | async-done | bytes 262160 | tf_op jit(solution)/shard_map/reduce_scatter | solution.py:73
  89.2 1.7 %broadcast_multiply_fusion = f32[2,4,64,128]{3,2,1,0:T(8,128)} fusion(f32[2,4,64,128]{3,2,1,0:T(8,128)} %reduce-scatter.2.cloned.1.call-done), kind=kLoop, calls=%fused_computation.9 | loop fusion | flops 65536 | bytes 524288 | tf_op jit(solution)/shard_map/mul | solution.py:76
  (7 shorter events, 0.1 us)
Async XLA Ops:
  6.5 82.7 %reduce-scatter.2.cloned.1.call-start = ((), (), s32[]{:S(2)}) async-start(), calls=%async_computation.1 | async-start | bytes 1310720 | tf_op jit(solution)/shard_map/reduce_scatter | solution.py:73
  7.5 6.4 %collective-permute-start = (f32[64,512]{1,0:T(8,128)S(1)}, f32[64,512]{1,0:T(8,128)S(1)}, u32[]{:S(2)}, u32[]{:S(2)}) collective-permute-start(f32[64,512]{1,0:T(8,128)S(1)} %slice.33), channel_id=1, source_target_pairs={{1,0},{2,1},{3,2},{5,4},{6,5},{7,6},{9,8},{10,9},{11,10},{13,12},{... | collective-permute-start | bytes 393224 | tf_op jit(solution)/shard_map/ppermute | solution.py:17
Sparse Core Ops, SparseCore 0:
  65.0 24.1 reduce-scatter.1
where the time goes:
time: 98 us; the launch traced here: 97.8 us
  blocking collectives  47.1 us (48%)
  waiting for transfers between devices  24.4 us (25%)
  between operations  13.5 us (14%)
  matrix products  5.6 us (6%)
  other arithmetic  3.79 us (4%)
  local copies, waits for them, and re-layouts  2.13 us (2%)
  starting transfers between devices  1.29 us (1%)
    all_gather x1, blocking collectives, body(): lax.all_gather(spectra_panel, 'pt', axis=2, tiled=True)  47.1 us
    reduce_scatter x1, waiting for transfers between devices, body(): lax.psum_scatter(partial_tiles, 'tm', scatter_dimension=3, tiled=True)  24.3 us
    dot_general x1, matrix products, body(): jnp.einsum('pbn,nc->pbc', blocks, table, precision=lax.Precision.HIGHEST)  4.15 us
  transfers between devices with their start and end apart: 2, of which 1 were waited for; matrix products, arithmetic and copies ran while one was open for 5% of the time, Pallas kernels for 0%

commit v1 on v0

v1 whole, which is shorter than its diff:
```python
import functools
import math

import jax
import jax.numpy as jnp
from jax import lax
from jax.experimental import pallas as pl
from jax.experimental.pallas import tpu as pltpu
from jax.sharding import PartitionSpec as P

SEGLEN = 1024
HALF = SEGLEN // 2
NFREQ = 4
COLS = 2 * NFREQ
LANES = 128
SERIES = [(-1) ** n / math.factorial(2 * n) for n in range(8)]
CONTRACT_LAST = (((1,), (1,)), ((), ()))
CONTRACT_FIRST = (((0,), (0,)), ((), ()))


def cosine_of(steps):
    wrapped = ((steps + HALF) & (SEGLEN - 1)) - HALF
    size = jnp.abs(wrapped)
    folded = size > HALF // 2
    size = jnp.where(folded, HALF - size, size)
    angle = size.astype(jnp.float32) * (2.0 * math.pi / SEGLEN)
    square = angle * angle
    value = jnp.full_like(square, SERIES[-1])
    for term in SERIES[-2::-1]:
        value = value * square + term
    return jnp.where(folded, -value, value)


def split(value):
    high = value.astype(jnp.bfloat16)
    low = (value - high.astype(jnp.float32)).astype(jnp.bfloat16)
    return high, low


def project_kernel(bins_ref, signals_ref, out_ref, held, sems):
    pairs, width, _ = held.shape
    points = width // 2
    copies = []
    for j in range(pairs):
        for h in range(2):
            copies.append(
                pltpu.make_async_copy(
                    signals_ref.at[:, pl.ds((j + pairs * h) * HALF, HALF)],
                    held.at[j, pl.ds(h * points, points), :],
                    sems.at[j, h],
                )
            )
            copies[-1].start()
    row = lax.broadcasted_iota(jnp.int32, (COLS, SEGLEN), 0)
    sample = lax.broadcasted_iota(jnp.int32, (COLS, SEGLEN), 1)
    bins = jnp.zeros((COLS, SEGLEN), jnp.int32)
    for f in range(NFREQ):
        bins = jnp.where(row % NFREQ == f, bins_ref[f], bins)
    window = 0.5 - 0.5 * cosine_of(sample)
    quarter = jnp.where(row >= NFREQ, SEGLEN // 4, 0)
    table = window * cosine_of(sample * bins + quarter)
    high, low = split(jnp.concatenate([table[:, :HALF], table[:, HALF:]], axis=0))
    both = jnp.concatenate([high, low], axis=0)
    first, second = [], []
    step = 4 if pairs % 4 == 0 else 1
    for j in range(0, pairs, step):
        for copy in copies[2 * j : 2 * (j + step)]:
            copy.wait()
        block = jnp.concatenate([held[j + q] for q in range(step)], axis=0)
        block_high, block_low = split(block)
        main = lax.dot_general(both, block_high, CONTRACT_LAST, preferred_element_type=jnp.float32)
        rest = lax.dot_general(high, block_low, CONTRACT_LAST, preferred_element_type=jnp.float32)
        sums = main[: 2 * COLS] + main[2 * COLS :] + rest
        for q in range(step):
            first.append(sums[:COLS, q * width : (q + 1) * width])
            second.append(sums[COLS:, q * width : (q + 1) * width])
    for j in range(pairs - 1):
        out_ref[j * COLS : (j + 1) * COLS, :] = first[j] + second[j + 1]
    lane = lax.broadcasted_iota(jnp.int32, (COLS, width), 1)
    wrap = jnp.where(lane < points, pltpu.roll(second[0], points, 1), 0.0)
    out_ref[(pairs - 1) * COLS : pairs * COLS, :] = first[pairs - 1] + wrap
    out_ref[pairs * COLS :, :] = second[0]


def project(signals, freq_bins):
    points, samples = signals.shape
    pairs = samples // HALF // 2
    return pl.pallas_call(
        project_kernel,
        out_shape=jax.ShapeDtypeStruct(((pairs + 1) * COLS, 2 * points), jnp.float32),
        in_specs=[pl.BlockSpec(memory_space=pltpu.SMEM), pl.BlockSpec(memory_space=pl.ANY)],
        out_specs=pl.BlockSpec(memory_space=pltpu.VMEM),
        scratch_shapes=[
            pltpu.VMEM((pairs, 2 * points, HALF), jnp.float32),
            pltpu.SemaphoreType.DMA((pairs, 2)),
        ],
        name="project",
    )(freq_bins, signals)


def tiles_kernel(chips, ratio, scale, place_ref, *refs):
    own_ref = refs[0]
    row_refs = refs[1:chips]
    column_refs = refs[chips : chips + chips * ratio]
    out_ref, left, right = refs[chips + chips * ratio :]
    chip, target, sub = place_ref[0], place_ref[1], place_ref[2]
    rows = left.shape[2]
    pairs = rows // COLS - 1
    points = LANES // 2

    def put(dst, src):
        for c in range(2):
            dst[c] = src[c * rows : (c + 1) * rows, :]

    put(left.at[chip], own_ref)
    for shift, ref in enumerate(row_refs, 1):
        put(left.at[lax.rem(chip + chips - shift, chips)], ref)
    for op, ref in enumerate(column_refs):
        mt, mb = divmod(op, ratio)
        source = lax.rem(target + chips - mt, chips)
        put(right.at[lax.rem(sub + ratio - mb, ratio), source], ref)

    lane = lax.broadcasted_iota(jnp.int32, (pairs, LANES), 1)
    low_half = lane < points
    last_row = (pairs - 1) * COLS
    low_lanes = lax.broadcasted_iota(jnp.int32, (COLS, LANES), 1) < points

    def finish(at):
        for t in range(2 * chips):
            here = at(t)
            value = here[last_row : last_row + COLS, :]
            if t + 1 < 2 * chips:
                extra = pltpu.roll(at(t + 1)[pairs * COLS :, :], points, 1)
                value = jnp.where(low_lanes, value, value + extra)
            else:
                value = jnp.where(low_lanes, value, 0.0)
            here[last_row : last_row + COLS, :] = value

    finish(lambda t: left.at[t // 2, t % 2])
    for b in range(ratio):
        finish(lambda t, b=b: right.at[b, t // 2, t % 2])

    def join(low, high):
        return (
            jnp.where(low_half, low, pltpu.roll(high, points, 1)),
            jnp.where(low_half, pltpu.roll(low, points, 1), high),
        )

    for f in range(NFREQ):
        lhs, rhs = [[], []], [[], []]
        for t in range(2 * chips):
            real, imag = (left.at[t // 2, t % 2][pl.ds(part * NFREQ + f, pairs, stride=COLS), :] for part in range(2))
            lhs[0] += join(real, imag)
            lhs[1] += join(imag, -real)
            for part in range(2):
                pick = pl.ds(part * NFREQ + f, pairs, stride=COLS)
                rhs[part] += join(*(right.at[b, t // 2, t % 2][pick, :] for b in range(2)))
        lhs_high, lhs_low = split(jnp.concatenate(lhs[0] + lhs[1], axis=0))
        rhs_high, rhs_low = split(jnp.concatenate(rhs[0] + rhs[1], axis=0))
        dot = functools.partial(
            lax.dot_general, dimension_numbers=CONTRACT_FIRST, preferred_element_type=jnp.float32
        )
        tile = dot(lhs_high, rhs_high) + (dot(lhs_high, rhs_low) + dot(lhs_low, rhs_high))
        tile = tile * scale
        out_ref[0, f] = tile[:points]
        out_ref[1, f] = tile[points:]


def body(signals, freq_bins):
    points, samples = signals.shape
    n_pt, n_tm = lax.axis_size("pt"), lax.axis_size("tm")
    ratio, chips = n_pt // n_tm, n_tm // 2
    where = lambda group, sub, chip, core: ((group * ratio + sub) * chips + chip) * 2 + core
    places = [
        (group, sub, chip, core)
        for group in range(n_tm)
        for sub in range(ratio)
        for chip in range(chips)
        for core in range(2)
    ]

    def permute(value, target):
        pairs = [(where(*place), where(*target(*place))) for place in places]
        return lax.ppermute(value, ("pt", "tm"), pairs)

    mine = project(signals, freq_bins)
    other = permute(mine, lambda g, s, x, c: (g, s, x, 1 - c))
    pt, tm = lax.axis_index("pt"), lax.axis_index("tm")
    is_first = tm % 2 == 0
    chip_block = jnp.concatenate(
        [jnp.where(is_first, mine, other), jnp.where(is_first, other, mine)], axis=0
    )
    row_blocks = [
        permute(chip_block, lambda g, s, x, c: (g, s, (x + m) % chips, c)) for m in range(1, chips)
    ]
    column_blocks = [
        permute(
            chip_block,
            lambda g, s, x, c: (2 * ((x + mt) % chips) + c, (s + mb) % ratio, g // 2, g % 2),
        )
        for mt in range(chips)
        for mb in range(ratio)
    ]
    place = jnp.stack([tm // 2, pt // ratio // 2, pt % ratio]).astype(jnp.int32)
    rows = mine.shape[0]
    segments = samples // HALF * n_tm - 1
    count = 1 + len(row_blocks) + len(column_blocks)
    return pl.pallas_call(
        functools.partial(tiles_kernel, chips, ratio, 1.0 / (segments * 0.375 * SEGLEN)),
        out_shape=jax.ShapeDtypeStruct((2, NFREQ, points, ratio * points), jnp.float32),
        in_specs=[pl.BlockSpec(memory_space=pltpu.SMEM)] + [pl.BlockSpec(memory_space=pltpu.VMEM)] * count,
        out_specs=pl.BlockSpec(memory_space=pltpu.VMEM),
        scratch_shapes=[
            pltpu.VMEM((chips, 2, rows, LANES), jnp.float32),
            pltpu.VMEM((ratio, chips, 2, rows, LANES), jnp.float32),
        ],
        name="tiles",
    )(place, chip_block, *row_blocks, *column_blocks)


def solution(mesh):
    in_specs = (P("pt", "tm"), P())
    out_specs = P(None, None, "pt", "tm")
    return jax.shard_map(body, mesh=mesh, in_specs=in_specs, out_specs=out_specs, check_vma=False)
```

time: 98 us -> 25.6 us (0.26)
  blocking collectives: 47.1 us -> 0 us
  waiting for transfers between devices: 24.4 us -> 4.23 us
  between operations: 13.5 us -> 0.1 us
  starting transfers between devices: 1.29 us -> 13.2 us
  Pallas kernels: 0 us -> 5.81 us
  matrix products: 5.6 us -> 0 us
  other arithmetic: 3.79 us -> 1.38 us
  local copies, waits for them, and re-layouts: 2.13 us -> 0.64 us
    all_gather x1 -> x0, blocking collectives: 47.1 us -> none  [body(): lax.all_gather(spectra_panel, 'pt', axis=2, tiled=True)]
    reduce_scatter x1 -> x0, waiting for transfers between devices: 24.3 us -> none  [body(): lax.psum_scatter(partial_tiles, 'tm', scatter_dimension=3, tiled=True)]
    ppermute x1 -> x6, starting transfers between devices: 1.29 us -> 13.2 us  [permute(): return lax.ppermute(value, ('pt', 'tm'), pairs)]
    pallas_call x0 -> x2, Pallas kernels: none -> 5.81 us  [the longest x1 3.52 us: project(): pl.pallas_call(project_kernel, out_shape=jax.ShapeDtypeStruct(((pairs + 1...]
    dot_general x4 -> x0, matrix products: 5.6 us -> none  [the longest x1 4.15 us: body(): jnp.einsum('pbn,nc->pbc', blocks, table, precision=lax.Precision.HIGHEST)]
    ppermute x1 -> x6, waiting for transfers between devices: 0.01 us -> 4.23 us  [permute(): return lax.ppermute(value, ('pt', 'tm'), pairs)]
    mul x3 -> x0, other arithmetic: 2.68 us -> none  [the longest x1 1.68 us: body(): return summed * scale]
    slice x3 -> x0, local copies, waits for them, and re-layouts: 1.29 us -> none  [the longest x1 0.91 us: body(): incoming = shifted(signals[:, :half_len], 'tm', -1)]
  transfers between devices with their start and end apart: 2 -> 6, of which waited for: 1 -> 2; matrix products, arithmetic and copies ran while one was open for 5% -> 2% of each run, Pallas kernels for 0% -> 0%
where the time goes in v1:
time: 25.6 us; the launch traced here: 25.4 us
  starting transfers between devices  13.2 us (52%)
  Pallas kernels  5.81 us (23%)
  waiting for transfers between devices  4.23 us (17%)
  other arithmetic  1.38 us (5%)
  local copies, waits for them, and re-layouts  0.64 us (2%)
    ppermute x6, starting transfers between devices, permute(): return lax.ppermute(value, ('pt', 'tm'), pairs)  13.2 us
    ppermute x6, waiting for transfers between devices, permute(): return lax.ppermute(value, ('pt', 'tm'), pairs)  4.23 us
    pallas_call x1, Pallas kernels, project(): pl.pallas_call(project_kernel, out_shape=jax.ShapeDtypeStruct(((pairs + 1...  3.52 us
    pallas_call x1, Pallas kernels, body(): pl.pallas_call(functools.partial(tiles_kernel, chips, ratio, 1.0 / (segme...  2.28 us
    select_n x1, other arithmetic, body(): jnp.where(is_first, mine, other)  0.77 us
    unnamed x12, local copies, waits for them, and re-layouts  0.64 us
    another operation x1, other arithmetic, body(): place = jnp.stack([tm // 2, pt // ratio // 2, pt % ratio]).astype(jnp.int32)  0.59 us
  transfers between devices with their start and end apart: 6, of which 2 were waited for; matrix products, arithmetic and copies ran while one was open for 2% of the time, Pallas kernels for 0%

profile of v1, /device:TPU:0, one launch (start us, length us, event | category | flops | bytes accessed | tf_op | source)
XLA Modules:
  0.0 25.4 jit_solution(17493693391656949059)
XLA Ops:
  0.0 3.5 %project.1 = f32[72,128]{1,0:T(8,128)} custom-call(s32[4]{0:T(128)} %bins_ref.1, f32[64,8192]{1,0:T(8,128)} %signals_ref.1), custom_call_target="tpu_custom_call" | custom-call | tf_op jit(solution)/shard_map/project/pallas_call | solution.py:88
  3.5 0.5 %collective-permute-start = (f32[72,128]{1,0:T(8,128)}, f32[72,128]{1,0:T(8,128)S(1)}, u32[]{:S(2)}, u32[]{:S(2)}) collective-permute-start(f32[72,128]{1,0:T(8,128)} %project.1), channel_id=1, source_target_pairs={{0,1},{1,0},{2,3},{3,2},{4,5},{5,4},{6,7},{7,6},{8,9},{9,8},{10,11... | collective-permute-start | bytes 110600 | tf_op jit(solution)/shard_map/ppermute | solution.py:184
  4.1 1.1 %collective-permute-done = f32[72,128]{1,0:T(8,128)S(1)} collective-permute-done((f32[72,128]{1,0:T(8,128)}, f32[72,128]{1,0:T(8,128)S(1)}, u32[]{:S(2)}, u32[]{:S(2)}) %collective-permute-start) | collective-permute-done | bytes 36896 | tf_op jit(solution)/shard_map/ppermute | solution.py:184
  5.1 0.8 %broadcast_select_fusion.1 = (f32[72,128]{1,0:T(8,128)S(1)}, f32[72,128]{1,0:T(8,128)S(1)}) fusion(f32[72,128]{1,0:T(8,128)} %project.1, f32[72,128]{1,0:T(8,128)S(1)} %collective-permute-done, pred[]{:T(512)S(6)} %eq.6), kind=kLoop, calls=%fused_computation.2 | loop fusion | flops 18432 | bytes 147457 | tf_op jit(solution)/shard_map/jit(_where)/select_n | solution.py:191
  5.9 0.0 copy-start
  5.9 4.9 %collective-permute-start.5 = (f32[144,128]{1,0:T(8,128)S(1)}, f32[144,128]{1,0:T(8,128)S(1)}, u32[]{:S(2)}, u32[]{:S(2)}) collective-permute-start(f32[144,128]{1,0:T(8,128)S(1)} %pad_maximum_fusion.refs_0_), channel_id=1, source_target_pairs={{0,20},{1,28},{2,4},{3,12},{4,16},{5,24},{6,0},{7,8},{8,21},{9,29}... | collective-permute-start | bytes 221192 | tf_op jit(solution)/shard_map/ppermute | solution.py:184
  10.9 1.5 %collective-permute-start.4 = (f32[144,128]{1,0:T(8,128)S(1)}, f32[144,128]{1,0:T(8,128)S(1)}, u32[]{:S(2)}, u32[]{:S(2)}) collective-permute-start(f32[144,128]{1,0:T(8,128)S(1)} %pad_maximum_fusion.refs_0_), channel_id=1, source_target_pairs={{0,16},{1,24},{2,0},{3,8},{4,20},{5,28},{6,4},{7,12},{8,17},{9,25}... | collective-permute-start | bytes 221192 | tf_op jit(solution)/shard_map/ppermute | solution.py:184
  12.4 0.5 %collective-permute-start.3 = (f32[144,128]{1,0:T(8,128)S(1)}, f32[144,128]{1,0:T(8,128)S(1)}, u32[]{:S(2)}, u32[]{:S(2)}) collective-permute-start(f32[144,128]{1,0:T(8,128)S(1)} %pad_maximum_fusion.refs_0_), channel_id=1, source_target_pairs={{0,4},{1,12},{2,20},{3,28},{4,0},{5,8},{6,16},{7,24},{8,5},{9,13},... | collective-permute-start | bytes 221192 | tf_op jit(solution)/shard_map/ppermute | solution.py:184
  12.9 0.7 %collective-permute-start.2 = (f32[144,128]{1,0:T(8,128)S(1)}, f32[144,128]{1,0:T(8,128)S(1)}, u32[]{:S(2)}, u32[]{:S(2)}) collective-permute-start(f32[144,128]{1,0:T(8,128)S(1)} %pad_maximum_fusion.refs_0_), channel_id=1, source_target_pairs={{0,0},{1,8},{2,16},{3,24},{4,4},{5,12},{6,20},{7,28},{8,1},{9,9},{... | collective-permute-start | bytes 221192 | tf_op jit(solution)/shard_map/ppermute | solution.py:184
  13.5 5.1 %collective-permute-start.1 = (f32[144,128]{1,0:T(8,128)S(1)}, f32[144,128]{1,0:T(8,128)S(1)}, u32[]{:S(2)}, u32[]{:S(2)}) collective-permute-start(f32[144,128]{1,0:T(8,128)S(1)} %pad_maximum_fusion.refs_0_), channel_id=1, source_target_pairs={{0,2},{1,3},{2,0},{3,1},{4,6},{5,7},{6,4},{7,5},{8,10},{9,11},{10,... | collective-permute-start | bytes 221192 | tf_op jit(solution)/shard_map/ppermute | solution.py:184
  18.6 0.6 %pad_add_fusion.place_ref = s32[3]{0:T(128)} fusion(s32[1]{0:T(128)} %bitcast.2, s32[1]{0:T(128)} %bitcast.1, s32[1]{0:T(128)} %bitcast), kind=kLoop, calls=%fused_computation.3 | loop fusion | flops 6 | bytes 24 | tf_op jit(solution)/shard_map/stack | solution.py:204
  19.2 0.0 collective-permute-done.5.refs_5_
  19.2 0.0 copy-start.1
  19.2 0.0 collective-permute-done.4.refs_4_
  19.2 0.0 copy-start.2
  19.2 0.0 collective-permute-done.3.refs_3_
  19.3 0.0 copy-start.3
  19.3 0.0 collective-permute-done.2.refs_2_
  19.3 0.0 copy-start.4
  19.3 3.1 %collective-permute-done.1.refs_1_ = f32[144,128]{1,0:T(8,128)S(1)} collective-permute-done((f32[144,128]{1,0:T(8,128)S(1)}, f32[144,128]{1,0:T(8,128)S(1)}, u32[]{:S(2)}, u32[]{:S(2)}) %collective-permute-start.1) | collective-permute-done | bytes 73760 | tf_op jit(solution)/shard_map/ppermute | solution.py:184
  22.4 0.0 copy-done
  22.4 0.0 copy-done.1
  22.4 0.0 copy-done.2
  22.4 0.0 copy-done.3
  22.4 0.0 copy-done.4
  22.5 0.0 copy-start.5
  22.5 0.6 %copy-done.5 = f32[144,128]{1,0:T(8,128)} copy-done((f32[144,128]{1,0:T(8,128)}, f32[144,128]{1,0:T(8,128)S(1)}, u32[]{:S(2)}) %copy-start.5) | copy-done | bytes 73752
  23.1 2.3 %tiles.1 = f32[2,4,64,128]{3,2,1,0:T(8,128)} custom-call(s32[3]{0:T(128)} %pad_add_fusion.place_ref, f32[144,128]{1,0:T(8,128)} %copy-done, f32[144,128]{1,0:T(8,128)} %copy-done.5, f32[144,128]{1,0:T(8,128)} %copy-done.4, f32[144,128]{1,0:T(8,128)} %copy-done.3, f32[144,128]{1,0:T(8,128)} %copy-done.2, f32[144,128]{1,0:T(8,128)} %copy-done.1), custom_call_target="tpu_custom_call" | custom-call | tf_op jit(solution)/shard_map/tiles/pallas_call | solution.py:208
  (1 shorter events, 0.0 us)
Async XLA Ops:
  3.5 1.6 %collective-permute-start = (f32[72,128]{1,0:T(8,128)}, f32[72,128]{1,0:T(8,128)S(1)}, u32[]{:S(2)}, u32[]{:S(2)}) collective-permute-start(f32[72,128]{1,0:T(8,128)} %project.1), channel_id=1, source_target_pairs={{0,1},{1,0},{2,3},{3,2},{4,5},{5,4},{6,7},{7,6},{8,9},{9,8},{10,11... | collective-permute-start | bytes 110600 | tf_op jit(solution)/shard_map/ppermute | solution.py:184
  5.9 16.5 %copy-start = (f32[144,128]{1,0:T(8,128)}, f32[144,128]{1,0:T(8,128)S(1)}, u32[]{:S(2)}) copy-start(f32[144,128]{1,0:T(8,128)S(1)} %pad_maximum_fusion.refs_0_) | copy-start | bytes 221188
  5.9 13.3 %collective-permute-start.5 = (f32[144,128]{1,0:T(8,128)S(1)}, f32[144,128]{1,0:T(8,128)S(1)}, u32[]{:S(2)}, u32[]{:S(2)}) collective-permute-start(f32[144,128]{1,0:T(8,128)S(1)} %pad_maximum_fusion.refs_0_), channel_id=1, source_target_pairs={{0,20},{1,28},{2,4},{3,12},{4,16},{5,24},{6,0},{7,8},{8,21},{9,29}... | collective-permute-start | bytes 221192 | tf_op jit(solution)/shard_map/ppermute | solution.py:184
  10.9 8.4 %collective-permute-start.4 = (f32[144,128]{1,0:T(8,128)S(1)}, f32[144,128]{1,0:T(8,128)S(1)}, u32[]{:S(2)}, u32[]{:S(2)}) collective-permute-start(f32[144,128]{1,0:T(8,128)S(1)} %pad_maximum_fusion.refs_0_), channel_id=1, source_target_pairs={{0,16},{1,24},{2,0},{3,8},{4,20},{5,28},{6,4},{7,12},{8,17},{9,25}... | collective-permute-start | bytes 221192 | tf_op jit(solution)/shard_map/ppermute | solution.py:184
  12.4 6.9 %collective-permute-start.3 = (f32[144,128]{1,0:T(8,128)S(1)}, f32[144,128]{1,0:T(8,128)S(1)}, u32[]{:S(2)}, u32[]{:S(2)}) collective-permute-start(f32[144,128]{1,0:T(8,128)S(1)} %pad_maximum_fusion.refs_0_), channel_id=1, source_target_pairs={{0,4},{1,12},{2,20},{3,28},{4,0},{5,8},{6,16},{7,24},{8,5},{9,13},... | collective-permute-start | bytes 221192 | tf_op jit(solution)/shard_map/ppermute | solution.py:184
  12.9 6.4 %collective-permute-start.2 = (f32[144,128]{1,0:T(8,128)S(1)}, f32[144,128]{1,0:T(8,128)S(1)}, u32[]{:S(2)}, u32[]{:S(2)}) collective-permute-start(f32[144,128]{1,0:T(8,128)S(1)} %pad_maximum_fusion.refs_0_), channel_id=1, source_target_pairs={{0,0},{1,8},{2,16},{3,24},{4,4},{5,12},{6,20},{7,28},{8,1},{9,9},{... | collective-permute-start | bytes 221192 | tf_op jit(solution)/shard_map/ppermute | solution.py:184
  13.5 8.9 %collective-permute-start.1 = (f32[144,128]{1,0:T(8,128)S(1)}, f32[144,128]{1,0:T(8,128)S(1)}, u32[]{:S(2)}, u32[]{:S(2)}) collective-permute-start(f32[144,128]{1,0:T(8,128)S(1)} %pad_maximum_fusion.refs_0_), channel_id=1, source_target_pairs={{0,2},{1,3},{2,0},{3,1},{4,6},{5,7},{6,4},{7,5},{8,10},{9,11},{10,... | collective-permute-start | bytes 221192 | tf_op jit(solution)/shard_map/ppermute | solution.py:184
  19.2 3.2 %copy-start.1 = (f32[144,128]{1,0:T(8,128)}, f32[144,128]{1,0:T(8,128)S(1)}, u32[]{:S(2)}) copy-start(f32[144,128]{1,0:T(8,128)S(1)} %collective-permute-done.5.refs_5_) | copy-start | bytes 221188
  19.2 3.2 %copy-start.2 = (f32[144,128]{1,0:T(8,128)}, f32[144,128]{1,0:T(8,128)S(1)}, u32[]{:S(2)}) copy-start(f32[144,128]{1,0:T(8,128)S(1)} %collective-permute-done.4.refs_4_) | copy-start | bytes 221188
  19.3 3.2 %copy-start.3 = (f32[144,128]{1,0:T(8,128)}, f32[144,128]{1,0:T(8,128)S(1)}, u32[]{:S(2)}) copy-start(f32[144,128]{1,0:T(8,128)S(1)} %collective-permute-done.3.refs_3_) | copy-start | bytes 221188
  19.3 3.2 %copy-start.4 = (f32[144,128]{1,0:T(8,128)}, f32[144,128]{1,0:T(8,128)S(1)}, u32[]{:S(2)}) copy-start(f32[144,128]{1,0:T(8,128)S(1)} %collective-permute-done.2.refs_2_) | copy-start | bytes 221188
  22.5 0.6 %copy-start.5 = (f32[144,128]{1,0:T(8,128)}, f32[144,128]{1,0:T(8,128)S(1)}, u32[]{:S(2)}) copy-start(f32[144,128]{1,0:T(8,128)S(1)} %collective-permute-done.1.refs_1_) | copy-start | bytes 221188

commit v2 on v1

--- a/solution.py
+++ b/solution.py
@@ -13,6 +13,7 @@
 NFREQ = 4
 COLS = 2 * NFREQ
 LANES = 128
+VMEM_LIMIT = 16 << 20
 SERIES = [(-1) ** n / math.factorial(2 * n) for n in range(8)]
 CONTRACT_LAST = (((1,), (1,)), ((), ()))
 CONTRACT_FIRST = (((0,), (0,)), ((), ()))
@@ -37,9 +38,11 @@
     return high, low
 
 
-def project_kernel(bins_ref, signals_ref, out_ref, held, sems):
+def project_kernel(bins_hbm, signals_ref, out_ref, held, sems, bins_ref, bins_sem):
     pairs, width, _ = held.shape
     points = width // 2
+    bins_copy = pltpu.make_async_copy(bins_hbm, bins_ref, bins_sem)
+    bins_copy.start()
     copies = []
     for j in range(pairs):
         for h in range(2):
@@ -53,10 +56,11 @@
             copies[-1].start()
     row = lax.broadcasted_iota(jnp.int32, (COLS, SEGLEN), 0)
     sample = lax.broadcasted_iota(jnp.int32, (COLS, SEGLEN), 1)
+    window = 0.5 - 0.5 * cosine_of(sample)
+    bins_copy.wait()
     bins = jnp.zeros((COLS, SEGLEN), jnp.int32)
     for f in range(NFREQ):
         bins = jnp.where(row % NFREQ == f, bins_ref[f], bins)
-    window = 0.5 - 0.5 * cosine_of(sample)
     quarter = jnp.where(row >= NFREQ, SEGLEN // 4, 0)
     table = window * cosine_of(sample * bins + quarter)
     high, low = split(jnp.concatenate([table[:, :HALF], table[:, HALF:]], axis=0))
@@ -88,37 +92,42 @@
     return pl.pallas_call(
         project_kernel,
         out_shape=jax.ShapeDtypeStruct(((pairs + 1) * COLS, 2 * points), jnp.float32),
-        in_specs=[pl.BlockSpec(memory_space=pltpu.SMEM), pl.BlockSpec(memory_space=pl.ANY)],
+        in_specs=[pl.BlockSpec(memory_space=pltpu.HBM)] * 2,
         out_specs=pl.BlockSpec(memory_space=pltpu.VMEM),
         scratch_shapes=[
             pltpu.VMEM((pairs, 2 * points, HALF), jnp.float32),
             pltpu.SemaphoreType.DMA((pairs, 2)),
+            pltpu.SMEM((NFREQ,), jnp.int32),
+            pltpu.SemaphoreType.DMA,
         ],
+        compiler_params=pltpu.CompilerParams(vmem_limit_bytes=VMEM_LIMIT),
         name="project",
     )(freq_bins, signals)
 
 
-def tiles_kernel(chips, ratio, scale, place_ref, *refs):
+def tiles_kernel(chips, ratio, scale, *refs):
     own_ref = refs[0]
     row_refs = refs[1:chips]
     column_refs = refs[chips : chips + chips * ratio]
     out_ref, left, right = refs[chips + chips * ratio :]
-    chip, target, sub = place_ref[0], place_ref[1], place_ref[2]
+    pt, tm = lax.axis_index("pt"), lax.axis_index("tm")
+    chip, target, sub = lax.div(tm, 2), lax.div(lax.div(pt, ratio), 2), lax.rem(pt, ratio)
     rows = left.shape[2]
     pairs = rows // COLS - 1
     points = LANES // 2
 
-    def put(dst, src):
+    def put(dst, src, sender):
         for c in range(2):
-            dst[c] = src[c * rows : (c + 1) * rows, :]
-
-    put(left.at[chip], own_ref)
+            dst[lax.rem(sender + c, 2)] = src[c * rows : (c + 1) * rows, :]
+
+    core, column_core = lax.rem(tm, 2), lax.rem(lax.div(pt, ratio), 2)
+    put(left.at[chip], own_ref, core)
     for shift, ref in enumerate(row_refs, 1):
-        put(left.at[lax.rem(chip + chips - shift, chips)], ref)
+        put(left.at[lax.rem(chip + chips - shift, chips)], ref, core)
     for op, ref in enumerate(column_refs):
         mt, mb = divmod(op, ratio)
         source = lax.rem(target + chips - mt, chips)
-        put(right.at[lax.rem(sub + ratio - mb, ratio), source], ref)
+        put(right.at[lax.rem(sub + ratio - mb, ratio), source], ref, column_core)
 
     lane = lax.broadcasted_iota(jnp.int32, (pairs, LANES), 1)
     low_half = lane < points
@@ -185,11 +194,7 @@
 
     mine = project(signals, freq_bins)
     other = permute(mine, lambda g, s, x, c: (g, s, x, 1 - c))
-    pt, tm = lax.axis_index("pt"), lax.axis_index("tm")
-    is_first = tm % 2 == 0
-    chip_block = jnp.concatenate(
-        [jnp.where(is_first, mine, other), jnp.where(is_first, other, mine)], axis=0
-    )
+    chip_block = jnp.concatenate([mine, other], axis=0)
     row_blocks = [
         permute(chip_block, lambda g, s, x, c: (g, s, (x + m) % chips, c)) for m in range(1, chips)
     ]
@@ -201,21 +206,21 @@
         for mt in range(chips)
         for mb in range(ratio)
     ]
-    place = jnp.stack([tm // 2, pt // ratio // 2, pt % ratio]).astype(jnp.int32)
     rows = mine.shape[0]
     segments = samples // HALF * n_tm - 1
     count = 1 + len(row_blocks) + len(column_blocks)
     return pl.pallas_call(
         functools.partial(tiles_kernel, chips, ratio, 1.0 / (segments * 0.375 * SEGLEN)),
         out_shape=jax.ShapeDtypeStruct((2, NFREQ, points, ratio * points), jnp.float32),
-        in_specs=[pl.BlockSpec(memory_space=pltpu.SMEM)] + [pl.BlockSpec(memory_space=pltpu.VMEM)] * count,
+        in_specs=[pl.BlockSpec(memory_space=pltpu.VMEM)] * count,
         out_specs=pl.BlockSpec(memory_space=pltpu.VMEM),
         scratch_shapes=[
             pltpu.VMEM((chips, 2, rows, LANES), jnp.float32),
             pltpu.VMEM((ratio, chips, 2, rows, LANES), jnp.float32),
         ],
+        compiler_params=pltpu.CompilerParams(vmem_limit_bytes=VMEM_LIMIT),
         name="tiles",
-    )(place, chip_block, *row_blocks, *column_blocks)
+    )(chip_block, *row_blocks, *column_blocks)
 
 
 def solution(mesh):

time: 25.6 us -> 23 us (0.90)
  Pallas kernels: 5.81 us -> 2.78 us
  local copies, waits for them, and re-layouts: 0.64 us -> 2.25 us
  other arithmetic: 1.38 us -> 0.01 us
  waiting for transfers between devices: 4.23 us -> 4.65 us
    pallas_call x1, Pallas kernels: 3.52 us -> 1.57 us  [project(): pl.pallas_call(project_kernel, out_shape=jax.ShapeDtypeStruct(((pairs + 1...]
    unnamed x12 -> x4, local copies, waits for them, and re-layouts: 0.64 us -> 2.25 us
    pallas_call x1, Pallas kernels: 2.28 us -> 1.22 us  [body(): pl.pallas_call(functools.partial(tiles_kernel, chips, ratio, 1.0 / (segme...]
    select_n x1 -> x0, other arithmetic: 0.77 us -> none  [body(): jnp.where(is_first, mine, other)]
    another operation x1 -> x0, other arithmetic: 0.59 us -> none  [body(): place = jnp.stack([tm // 2, pt // ratio // 2, pt % ratio]).astype(jnp.int32)]
    ppermute x6, waiting for transfers between devices: 4.23 us -> 4.65 us  [permute(): return lax.ppermute(value, ('pt', 'tm'), pairs)]
  transfers between devices with their start and end apart: 6 -> 6, of which waited for: 2 -> 2; matrix products, arithmetic and copies ran while one was open for 2% -> 0% of each run, Pallas kernels for 0% -> 0%
where the time goes in v2:
time: 23 us; the launch traced here: 22.9 us
  starting transfers between devices  13.2 us (57%)
  waiting for transfers between devices  4.65 us (20%)
  Pallas kernels  2.78 us (12%)
  local copies, waits for them, and re-layouts  2.25 us (10%)
    ppermute x6, starting transfers between devices, permute(): return lax.ppermute(value, ('pt', 'tm'), pairs)  13.2 us
    ppermute x6, waiting for transfers between devices, permute(): return lax.ppermute(value, ('pt', 'tm'), pairs)  4.65 us
    unnamed x4, local copies, waits for them, and re-layouts  2.25 us
    pallas_call x1, Pallas kernels, project(): pl.pallas_call(project_kernel, out_shape=jax.ShapeDtypeStruct(((pairs + 1...  1.57 us
    pallas_call x1, Pallas kernels, body(): pl.pallas_call(functools.partial(tiles_kernel, chips, ratio, 1.0 / (segme...  1.22 us
  transfers between devices with their start and end apart: 6, of which 2 were waited for; matrix products, arithmetic and copies ran while one was open for 0% of the time, Pallas kernels for 0%

profile of v2, /device:TPU:0, one launch (start us, length us, event | category | flops | bytes accessed | tf_op | source)
XLA Modules:
  0.0 22.9 jit_solution(17400046422239511570)
XLA Ops:
  0.0 0.0 copy-start
  0.0 1.6 %copy-done = f32[64,8192]{1,0:T(8,128)S(1)} copy-done((f32[64,8192]{1,0:T(8,128)S(1)}, f32[64,8192]{1,0:T(8,128)}, u32[]{:S(2)}) %copy-start) | copy-done | bytes 2097176
  1.6 0.0 copy-start.1
  1.6 0.7 %copy-done.1 = s32[4]{0:T(128)S(1)} copy-done((s32[4]{0:T(128)S(1)}, s32[4]{0:T(128)}, u32[]{:S(2)}) %copy-start.1) | copy-done | bytes 40
  2.2 1.6 %project.1 = f32[72,128]{1,0:T(8,128)S(1)} custom-call(s32[4]{0:T(128)S(1)} %copy-done.1, f32[64,8192]{1,0:T(8,128)S(1)} %copy-done), custom_call_target="tpu_custom_call" | custom-call | tf_op jit(solution)/shard_map/project/pallas_call | solution.py:92
  3.8 0.5 %collective-permute-start = (f32[72,128]{1,0:T(8,128)S(1)}, f32[72,128]{1,0:T(8,128)S(1)}, u32[]{:S(2)}, u32[]{:S(2)}) collective-permute-start(f32[72,128]{1,0:T(8,128)S(1)} %project.1), channel_id=1, source_target_pairs={{0,1},{1,0},{2,3},{3,2},{4,5},{5,4},{6,7},{7,6},{8,9},{9,8},{10,11... | collective-permute-start | bytes 110600 | tf_op jit(solution)/shard_map/ppermute | solution.py:193
  4.3 0.9 %collective-permute-done = f32[72,128]{1,0:T(8,128)S(1)} collective-permute-done((f32[72,128]{1,0:T(8,128)S(1)}, f32[72,128]{1,0:T(8,128)S(1)}, u32[]{:S(2)}, u32[]{:S(2)}) %collective-permute-start) | collective-permute-done | bytes 36896 | tf_op jit(solution)/shard_map/ppermute | solution.py:193
  5.2 4.9 %collective-permute-start.5 = (f32[144,128]{1,0:T(8,128)S(1)}, f32[144,128]{1,0:T(8,128)S(1)}, u32[]{:S(2)}, u32[]{:S(2)}) collective-permute-start(f32[144,128]{1,0:T(8,128)S(1)} %pad_maximum_fusion.refs_0_), channel_id=1, source_target_pairs={{0,20},{1,28},{2,4},{3,12},{4,16},{5,24},{6,0},{7,8},{8,21},{9,29}... | collective-permute-start | bytes 221192 | tf_op jit(solution)/shard_map/ppermute | solution.py:193
  10.1 1.5 %collective-permute-start.4 = (f32[144,128]{1,0:T(8,128)S(1)}, f32[144,128]{1,0:T(8,128)S(1)}, u32[]{:S(2)}, u32[]{:S(2)}) collective-permute-start(f32[144,128]{1,0:T(8,128)S(1)} %pad_maximum_fusion.refs_0_), channel_id=1, source_target_pairs={{0,16},{1,24},{2,0},{3,8},{4,20},{5,28},{6,4},{7,12},{8,17},{9,25}... | collective-permute-start | bytes 221192 | tf_op jit(solution)/shard_map/ppermute | solution.py:193
  11.6 0.5 %collective-permute-start.3 = (f32[144,128]{1,0:T(8,128)S(1)}, f32[144,128]{1,0:T(8,128)S(1)}, u32[]{:S(2)}, u32[]{:S(2)}) collective-permute-start(f32[144,128]{1,0:T(8,128)S(1)} %pad_maximum_fusion.refs_0_), channel_id=1, source_target_pairs={{0,4},{1,12},{2,20},{3,28},{4,0},{5,8},{6,16},{7,24},{8,5},{9,13},... | collective-permute-start | bytes 221192 | tf_op jit(solution)/shard_map/ppermute | solution.py:193
  12.1 0.7 %collective-permute-start.2 = (f32[144,128]{1,0:T(8,128)S(1)}, f32[144,128]{1,0:T(8,128)S(1)}, u32[]{:S(2)}, u32[]{:S(2)}) collective-permute-start(f32[144,128]{1,0:T(8,128)S(1)} %pad_maximum_fusion.refs_0_), channel_id=1, source_target_pairs={{0,0},{1,8},{2,16},{3,24},{4,4},{5,12},{6,20},{7,28},{8,1},{9,9},{... | collective-permute-start | bytes 221192 | tf_op jit(solution)/shard_map/ppermute | solution.py:193
  12.8 5.1 %collective-permute-start.1 = (f32[144,128]{1,0:T(8,128)S(1)}, f32[144,128]{1,0:T(8,128)S(1)}, u32[]{:S(2)}, u32[]{:S(2)}) collective-permute-start(f32[144,128]{1,0:T(8,128)S(1)} %pad_maximum_fusion.refs_0_), channel_id=1, source_target_pairs={{0,2},{1,3},{2,0},{3,1},{4,6},{5,7},{6,4},{7,5},{8,10},{9,11},{10,... | collective-permute-start | bytes 221192 | tf_op jit(solution)/shard_map/ppermute | solution.py:193
  17.9 0.0 collective-permute-done.5.refs_5_
  17.9 0.0 collective-permute-done.4.refs_4_
  17.9 0.0 collective-permute-done.3.refs_3_
  17.9 0.0 collective-permute-done.2.refs_2_
  17.9 3.8 %collective-permute-done.1.refs_1_ = f32[144,128]{1,0:T(8,128)S(1)} collective-permute-done((f32[144,128]{1,0:T(8,128)S(1)}, f32[144,128]{1,0:T(8,128)S(1)}, u32[]{:S(2)}, u32[]{:S(2)}) %collective-permute-start.1) | collective-permute-done | bytes 73760 | tf_op jit(solution)/shard_map/ppermute | solution.py:193
  21.7 1.2 %tiles.1 = f32[2,4,64,128]{3,2,1,0:T(8,128)} custom-call(f32[144,128]{1,0:T(8,128)S(1)} %pad_maximum_fusion.refs_0_, f32[144,128]{1,0:T(8,128)S(1)} %collective-permute-done.1.refs_1_, f32[144,128]{1,0:T(8,128)S(1)} %collective-permute-done.2.refs_2_, f32[144,128]{1,0:T(8,128)S(1)} %collective-permute-done.3.refs_3_, ...), custom_call_target="tpu_custom_call" | custom-call | tf_op jit(solution)/shard_map/tiles/pallas_call | solution.py:212
  (1 shorter events, 0.0 us)
Async XLA Ops:
  0.0 1.6 %copy-start = (f32[64,8192]{1,0:T(8,128)S(1)}, f32[64,8192]{1,0:T(8,128)}, u32[]{:S(2)}) copy-start(f32[64,8192]{1,0:T(8,128)} %signals_ref.1) | copy-start | bytes 6291460
  1.6 0.7 %copy-start.1 = (s32[4]{0:T(128)S(1)}, s32[4]{0:T(128)}, u32[]{:S(2)}) copy-start(s32[4]{0:T(128)} %bins_hbm.1) | copy-start | bytes 52
  3.8 1.4 %collective-permute-start = (f32[72,128]{1,0:T(8,128)S(1)}, f32[72,128]{1,0:T(8,128)S(1)}, u32[]{:S(2)}, u32[]{:S(2)}) collective-permute-start(f32[72,128]{1,0:T(8,128)S(1)} %project.1), channel_id=1, source_target_pairs={{0,1},{1,0},{2,3},{3,2},{4,5},{5,4},{6,7},{7,6},{8,9},{9,8},{10,11... | collective-permute-start | bytes 110600 | tf_op jit(solution)/shard_map/ppermute | solution.py:193
  5.2 12.7 %collective-permute-start.5 = (f32[144,128]{1,0:T(8,128)S(1)}, f32[144,128]{1,0:T(8,128)S(1)}, u32[]{:S(2)}, u32[]{:S(2)}) collective-permute-start(f32[144,128]{1,0:T(8,128)S(1)} %pad_maximum_fusion.refs_0_), channel_id=1, source_target_pairs={{0,20},{1,28},{2,4},{3,12},{4,16},{5,24},{6,0},{7,8},{8,21},{9,29}... | collective-permute-start | bytes 221192 | tf_op jit(solution)/shard_map/ppermute | solution.py:193
  10.1 7.8 %collective-permute-start.4 = (f32[144,128]{1,0:T(8,128)S(1)}, f32[144,128]{1,0:T(8,128)S(1)}, u32[]{:S(2)}, u32[]{:S(2)}) collective-permute-start(f32[144,128]{1,0:T(8,128)S(1)} %pad_maximum_fusion.refs_0_), channel_id=1, source_target_pairs={{0,16},{1,24},{2,0},{3,8},{4,20},{5,28},{6,4},{7,12},{8,17},{9,25}... | collective-permute-start | bytes 221192 | tf_op jit(solution)/shard_map/ppermute | solution.py:193
  11.6 6.3 %collective-permute-start.3 = (f32[144,128]{1,0:T(8,128)S(1)}, f32[144,128]{1,0:T(8,128)S(1)}, u32[]{:S(2)}, u32[]{:S(2)}) collective-permute-start(f32[144,128]{1,0:T(8,128)S(1)} %pad_maximum_fusion.refs_0_), channel_id=1, source_target_pairs={{0,4},{1,12},{2,20},{3,28},{4,0},{5,8},{6,16},{7,24},{8,5},{9,13},... | collective-permute-start | bytes 221192 | tf_op jit(solution)/shard_map/ppermute | solution.py:193
  12.1 5.8 %collective-permute-start.2 = (f32[144,128]{1,0:T(8,128)S(1)}, f32[144,128]{1,0:T(8,128)S(1)}, u32[]{:S(2)}, u32[]{:S(2)}) collective-permute-start(f32[144,128]{1,0:T(8,128)S(1)} %pad_maximum_fusion.refs_0_), channel_id=1, source_target_pairs={{0,0},{1,8},{2,16},{3,24},{4,4},{5,12},{6,20},{7,28},{8,1},{9,9},{... | collective-permute-start | bytes 221192 | tf_op jit(solution)/shard_map/ppermute | solution.py:193
  12.8 8.9 %collective-permute-start.1 = (f32[144,128]{1,0:T(8,128)S(1)}, f32[144,128]{1,0:T(8,128)S(1)}, u32[]{:S(2)}, u32[]{:S(2)}) collective-permute-start(f32[144,128]{1,0:T(8,128)S(1)} %pad_maximum_fusion.refs_0_), channel_id=1, source_target_pairs={{0,2},{1,3},{2,0},{3,1},{4,6},{5,7},{6,4},{7,5},{8,10},{9,11},{10,... | collective-permute-start | bytes 221192 | tf_op jit(solution)/shard_map/ppermute | solution.py:193

commit v3 on v2

--- a/solution.py
+++ b/solution.py
@@ -14,6 +14,10 @@
 COLS = 2 * NFREQ
 LANES = 128
 VMEM_LIMIT = 16 << 20
+COLUMN_ROUNDS = (
+    ((3, 1, 2, 0), (2, 3, 0, 1), (3, 1, 0, 2), (2, 3, 1, 0)),
+    ((2, 0, 1, 3), (1, 0, 2, 3), (2, 0, 1, 3), (0, 1, 3, 2)),
+)
 SERIES = [(-1) ** n / math.factorial(2 * n) for n in range(8)]
 CONTRACT_LAST = (((1,), (1,)), ((), ()))
 CONTRACT_FIRST = (((0,), (0,)), ((), ()))
@@ -86,6 +90,10 @@
     out_ref[pairs * COLS :, :] = second[0]
 
 
+def in_hbm(value):
+    return pltpu.with_memory_space_constraint(value, pltpu.HBM)
+
+
 def project(signals, freq_bins):
     points, samples = signals.shape
     pairs = samples // HALF // 2
@@ -102,16 +110,31 @@
         ],
         compiler_params=pltpu.CompilerParams(vmem_limit_bytes=VMEM_LIMIT),
         name="project",
-    )(freq_bins, signals)
-
-
-def tiles_kernel(chips, ratio, scale, *refs):
+    )(in_hbm(freq_bins), in_hbm(signals))
+
+
+def lookup(values, device):
+    total = 0
+    for bit in range(max(values).bit_length()):
+        word = 0
+        for start in range(0, len(values), 32):
+            packed = sum((v >> bit & 1) << n for n, v in enumerate(values[start : start + 32]))
+            packed -= (packed >> 31) << 32
+            here = jnp.int32(packed)
+            word = here if start == 0 else jnp.where(device >= start, here, word)
+        total += (lax.shift_right_logical(word, lax.rem(device, 32)) & 1) << bit
+    return total
+
+
+def tiles_kernel(rounds, chips, ratio, scale, *refs):
     own_ref = refs[0]
-    row_refs = refs[1:chips]
-    column_refs = refs[chips : chips + chips * ratio]
-    out_ref, left, right = refs[chips + chips * ratio :]
-    pt, tm = lax.axis_index("pt"), lax.axis_index("tm")
-    chip, target, sub = lax.div(tm, 2), lax.div(lax.div(pt, ratio), 2), lax.rem(pt, ratio)
+    count = sum(1 if is_row else ratio for is_row, _ in rounds)
+    round_refs = list(refs[1 : 1 + count])
+    out_ref, left, right = refs[1 + count :]
+    tm = lax.axis_index("tm")
+    pt = lax.axis_index("pt")
+    device = pt * lax.axis_size("tm") + tm
+    sub = lax.rem(pt, ratio)
     rows = left.shape[2]
     pairs = rows // COLS - 1
     points = LANES // 2
@@ -120,14 +143,16 @@
         for c in range(2):
             dst[lax.rem(sender + c, 2)] = src[c * rows : (c + 1) * rows, :]
 
-    core, column_core = lax.rem(tm, 2), lax.rem(lax.div(pt, ratio), 2)
-    put(left.at[chip], own_ref, core)
-    for shift, ref in enumerate(row_refs, 1):
-        put(left.at[lax.rem(chip + chips - shift, chips)], ref, core)
-    for op, ref in enumerate(column_refs):
-        mt, mb = divmod(op, ratio)
-        source = lax.rem(target + chips - mt, chips)
-        put(right.at[lax.rem(sub + ratio - mb, ratio), source], ref, column_core)
+    put(left.at[lax.div(tm, 2)], own_ref, lax.rem(tm, 2))
+    for is_row, targets in rounds:
+        sources = [targets.index(d) for d in range(len(targets))]
+        core = lookup([d % 2 for d in sources], device)
+        chip = lookup([d // 2 % chips for d in sources], device)
+        if is_row:
+            put(left.at[chip], round_refs.pop(0), core)
+        else:
+            for m in range(ratio):
+                put(right.at[lax.rem(sub + ratio - m, ratio), chip], round_refs.pop(0), core)
 
     lane = lax.broadcasted_iota(jnp.int32, (pairs, LANES), 1)
     low_half = lane < points
@@ -175,44 +200,60 @@
         out_ref[1, f] = tile[points:]
 
 
+def plan_rounds(chips, ratio):
+    cores = 2 * chips
+    devices = [
+        (group, sub, chip, core)
+        for group in range(cores)
+        for sub in range(ratio)
+        for chip in range(chips)
+        for core in range(2)
+    ]
+    number = {place: n for n, place in enumerate(devices)}
+    rounds = []
+    for m in range(chips):
+        if chips == len(COLUMN_ROUNDS):
+            groups = COLUMN_ROUNDS[m]
+        else:
+            order = [2 * ((x + m) % chips) + c for x in range(chips) for c in range(2)]
+            groups = [order] * cores
+        rounds.append((False, [
+            number[groups[g][2 * x + c], s, g // 2, g % 2] for g, s, x, c in devices
+        ]))
+    for m in range(1, chips):
+        rounds.append((True, [number[g, s, (x + m) % chips, c] for g, s, x, c in devices]))
+    return rounds
+
+
 def body(signals, freq_bins):
     points, samples = signals.shape
     n_pt, n_tm = lax.axis_size("pt"), lax.axis_size("tm")
     ratio, chips = n_pt // n_tm, n_tm // 2
-    where = lambda group, sub, chip, core: ((group * ratio + sub) * chips + chip) * 2 + core
-    places = [
-        (group, sub, chip, core)
-        for group in range(n_tm)
-        for sub in range(ratio)
-        for chip in range(chips)
-        for core in range(2)
-    ]
-
-    def permute(value, target):
-        pairs = [(where(*place), where(*target(*place))) for place in places]
-        return lax.ppermute(value, ("pt", "tm"), pairs)
+
+    def permute(value, targets):
+        return lax.ppermute(value, ("pt", "tm"), list(enumerate(targets)))
+
+    def to_sub(value, m):
+        pairs = [(n, n // ratio * ratio + (n + m) % ratio) for n in range(n_pt)]
+        return lax.ppermute(value, "pt", pairs)
 
     mine = project(signals, freq_bins)
-    other = permute(mine, lambda g, s, x, c: (g, s, x, 1 - c))
+    other = permute(mine, [n ^ 1 for n in range(n_pt * n_tm)])
     chip_block = jnp.concatenate([mine, other], axis=0)
-    row_blocks = [
-        permute(chip_block, lambda g, s, x, c: (g, s, (x + m) % chips, c)) for m in range(1, chips)
-    ]
-    column_blocks = [
-        permute(
-            chip_block,
-            lambda g, s, x, c: (2 * ((x + mt) % chips) + c, (s + mb) % ratio, g // 2, g % 2),
-        )
-        for mt in range(chips)
-        for mb in range(ratio)
-    ]
+    rounds = plan_rounds(chips, ratio)
+    blocks = []
+    for is_row, targets in rounds:
+        blocks.append(permute(chip_block, targets))
+        if not is_row:
+            column = blocks[-1]
+            blocks += [to_sub(column, m) for m in range(1, ratio)]
     rows = mine.shape[0]
     segments = samples // HALF * n_tm - 1
-    count = 1 + len(row_blocks) + len(column_blocks)
+    scale = 1.0 / (segments * 0.375 * SEGLEN)
     return pl.pallas_call(
-        functools.partial(tiles_kernel, chips, ratio, 1.0 / (segments * 0.375 * SEGLEN)),
+        functools.partial(tiles_kernel, rounds, chips, ratio, scale),
         out_shape=jax.ShapeDtypeStruct((2, NFREQ, points, ratio * points), jnp.float32),
-        in_specs=[pl.BlockSpec(memory_space=pltpu.VMEM)] * count,
+        in_specs=[pl.BlockSpec(memory_space=pltpu.VMEM)] * (1 + len(blocks)),
         out_specs=pl.BlockSpec(memory_space=pltpu.VMEM),
         scratch_shapes=[
             pltpu.VMEM((chips, 2, rows, LANES), jnp.float32),
@@ -220,7 +261,7 @@
         ],
         compiler_params=pltpu.CompilerParams(vmem_limit_bytes=VMEM_LIMIT),
         name="tiles",
-    )(chip_block, *row_blocks, *column_blocks)
+    )(chip_block, *blocks)
 
 
 def solution(mesh):

time: 23 us -> 17.8 us (0.77)
  starting transfers between devices: 13.2 us -> 10.3 us
  local copies, waits for them, and re-layouts: 2.25 us -> 0 us
  waiting for transfers between devices: 4.65 us -> 3.83 us
  Pallas kernels: 2.78 us -> 3.47 us
    ppermute x6, starting transfers between devices: 13.2 us -> 10.3 us  [the longest x4 7.4 us: permute(): return lax.ppermute(value, ('pt', 'tm'), list(enumerate(targets)))]
    unnamed x4 -> x0, local copies, waits for them, and re-layouts: 2.25 us -> none
    ppermute x6, waiting for transfers between devices: 4.65 us -> 3.83 us  [the longest x2 2.55 us: to_sub(): return lax.ppermute(value, 'pt', pairs)]
    pallas_call x1, Pallas kernels: 1.57 us -> 2.26 us  [project(): pl.pallas_call(project_kernel, out_shape=jax.ShapeDtypeStruct(((pairs + 1...]
  transfers between devices with their start and end apart: 6 -> 6, of which waited for: 2 -> 4; matrix products, arithmetic and copies ran while one was open for 0% -> 0% of each run, Pallas kernels for 0% -> 0%
where the time goes in v3:
time: 17.8 us; the launch traced here: 17.6 us
  starting transfers between devices  10.3 us (58%)
  waiting for transfers between devices  3.83 us (22%)
  Pallas kernels  3.47 us (19%)
    ppermute x4, starting transfers between devices, permute(): return lax.ppermute(value, ('pt', 'tm'), list(enumerate(targets)))  7.4 us
    ppermute x2, starting transfers between devices, to_sub(): return lax.ppermute(value, 'pt', pairs)  2.91 us
    ppermute x2, waiting for transfers between devices, to_sub(): return lax.ppermute(value, 'pt', pairs)  2.55 us
    pallas_call x1, Pallas kernels, project(): pl.pallas_call(project_kernel, out_shape=jax.ShapeDtypeStruct(((pairs + 1...  2.26 us
    ppermute x4, waiting for transfers between devices, permute(): return lax.ppermute(value, ('pt', 'tm'), list(enumerate(targets)))  1.28 us
    pallas_call x1, Pallas kernels, body(): pl.pallas_call(functools.partial(tiles_kernel, rounds, chips, ratio, scal...  1.22 us
  transfers between devices with their start and end apart: 6, of which 4 were waited for; matrix products, arithmetic and copies ran while one was open for 0% of the time, Pallas kernels for 0%

profile of v3, /device:TPU:0, one launch (start us, length us, event | category | flops | bytes accessed | tf_op | source)
XLA Modules:
  0.0 17.6 jit_solution(16706848256790802727)
XLA Ops:
  0.0 2.3 %project.1 = f32[72,128]{1,0:T(8,128)S(1)} custom-call(s32[4]{0:T(128)} %bins_hbm.1, f32[64,8192]{1,0:T(8,128)} %signals_ref.1), custom_call_target="tpu_custom_call" | custom-call | tf_op jit(solution)/shard_map/project/pallas_call | solution.py:100
  2.3 0.5 %collective-permute-start = (f32[72,128]{1,0:T(8,128)S(1)}, f32[72,128]{1,0:T(8,128)S(1)}, u32[]{:S(2)}, u32[]{:S(2)}) collective-permute-start(f32[72,128]{1,0:T(8,128)S(1)} %project.1), channel_id=1, source_target_pairs={{0,1},{1,0},{2,3},{3,2},{4,5},{5,4},{6,7},{7,6},{8,9},{9,8},{10,11... | collective-permute-start | bytes 110600 | tf_op jit(solution)/shard_map/ppermute | solution.py:234
  2.8 0.9 %collective-permute-done = f32[72,128]{1,0:T(8,128)S(1)} collective-permute-done((f32[72,128]{1,0:T(8,128)S(1)}, f32[72,128]{1,0:T(8,128)S(1)}, u32[]{:S(2)}, u32[]{:S(2)}) %collective-permute-start) | collective-permute-done | bytes 36896 | tf_op jit(solution)/shard_map/ppermute | solution.py:234
  3.7 3.9 %collective-permute-start.3 = (f32[144,128]{1,0:T(8,128)S(1)}, f32[144,128]{1,0:T(8,128)S(1)}, u32[]{:S(2)}, u32[]{:S(2)}) collective-permute-start(f32[144,128]{1,0:T(8,128)S(1)} %pad_maximum_fusion.refs_0_), channel_id=1, source_target_pairs={{0,16},{1,0},{2,8},{3,24},{4,20},{5,4},{6,12},{7,28},{8,9},{9,1},{... | collective-permute-start | bytes 221192 | tf_op jit(solution)/shard_map/ppermute | solution.py:234
  7.6 1.9 %collective-permute-start.1 = (f32[144,128]{1,0:T(8,128)S(1)}, f32[144,128]{1,0:T(8,128)S(1)}, u32[]{:S(2)}, u32[]{:S(2)}) collective-permute-start(f32[144,128]{1,0:T(8,128)S(1)} %pad_maximum_fusion.refs_0_), channel_id=1, source_target_pairs={{0,24},{1,8},{2,16},{3,0},{4,28},{5,12},{6,20},{7,4},{8,17},{9,25}... | collective-permute-start | bytes 221192 | tf_op jit(solution)/shard_map/ppermute | solution.py:234
  9.5 1.0 %collective-permute-start.5 = (f32[144,128]{1,0:T(8,128)S(1)}, f32[144,128]{1,0:T(8,128)S(1)}, u32[]{:S(2)}, u32[]{:S(2)}) collective-permute-start(f32[144,128]{1,0:T(8,128)S(1)} %pad_maximum_fusion.refs_0_), channel_id=1, source_target_pairs={{0,2},{1,3},{2,0},{3,1},{4,6},{5,7},{6,4},{7,5},{8,10},{9,11},{10,... | collective-permute-start | bytes 221192 | tf_op jit(solution)/shard_map/ppermute | solution.py:234
  10.5 0.0 collective-permute-done.3.refs_3_
  10.5 1.5 %collective-permute-start.4 = (f32[144,128]{1,0:T(8,128)S(1)}, f32[144,128]{1,0:T(8,128)S(1)}, u32[]{:S(2)}, u32[]{:S(2)}) collective-permute-start(f32[144,128]{1,0:T(8,128)S(1)} %collective-permute-done.3.refs_3_), channel_id=1, source_target_pairs={{0,4},{4,0},{8,12},{12,8},{16,20},{20,16},{24,28},{28,24},{1,5},{5... | collective-permute-start | bytes 221192 | tf_op jit(solution)/shard_map/ppermute | solution.py:238
  12.1 0.0 collective-permute-done.1.refs_1_
  12.1 1.4 %collective-permute-start.2 = (f32[144,128]{1,0:T(8,128)S(1)}, f32[144,128]{1,0:T(8,128)S(1)}, u32[]{:S(2)}, u32[]{:S(2)}) collective-permute-start(f32[144,128]{1,0:T(8,128)S(1)} %collective-permute-done.1.refs_1_), channel_id=1, source_target_pairs={{0,4},{4,0},{8,12},{12,8},{16,20},{20,16},{24,28},{28,24},{1,5},{5... | collective-permute-start | bytes 221192 | tf_op jit(solution)/shard_map/ppermute | solution.py:238
  13.5 0.4 %collective-permute-done.5.refs_5_ = f32[144,128]{1,0:T(8,128)S(1)} collective-permute-done((f32[144,128]{1,0:T(8,128)S(1)}, f32[144,128]{1,0:T(8,128)S(1)}, u32[]{:S(2)}, u32[]{:S(2)}) %collective-permute-start.5) | collective-permute-done | bytes 73760 | tf_op jit(solution)/shard_map/ppermute | solution.py:234
  13.9 1.5 %collective-permute-done.4.refs_4_ = f32[144,128]{1,0:T(8,128)S(1)} collective-permute-done((f32[144,128]{1,0:T(8,128)S(1)}, f32[144,128]{1,0:T(8,128)S(1)}, u32[]{:S(2)}, u32[]{:S(2)}) %collective-permute-start.4) | collective-permute-done | bytes 73760 | tf_op jit(solution)/shard_map/ppermute | solution.py:238
  15.3 1.1 %collective-permute-done.2.refs_2_ = f32[144,128]{1,0:T(8,128)S(1)} collective-permute-done((f32[144,128]{1,0:T(8,128)S(1)}, f32[144,128]{1,0:T(8,128)S(1)}, u32[]{:S(2)}, u32[]{:S(2)}) %collective-permute-start.2) | collective-permute-done | bytes 73760 | tf_op jit(solution)/shard_map/ppermute | solution.py:238
  16.4 1.2 %tiles.1 = f32[2,4,64,128]{3,2,1,0:T(8,128)} custom-call(f32[144,128]{1,0:T(8,128)S(1)} %pad_maximum_fusion.refs_0_, f32[144,128]{1,0:T(8,128)S(1)} %collective-permute-done.1.refs_1_, f32[144,128]{1,0:T(8,128)S(1)} %collective-permute-done.2.refs_2_, f32[144,128]{1,0:T(8,128)S(1)} %collective-permute-done.3.refs_3_, ...), custom_call_target="tpu_custom_call" | custom-call | tf_op jit(solution)/shard_map/tiles/pallas_call | solution.py:253
  (1 shorter events, 0.0 us)
Async XLA Ops:
  2.3 1.4 %collective-permute-start = (f32[72,128]{1,0:T(8,128)S(1)}, f32[72,128]{1,0:T(8,128)S(1)}, u32[]{:S(2)}, u32[]{:S(2)}) collective-permute-start(f32[72,128]{1,0:T(8,128)S(1)} %project.1), channel_id=1, source_target_pairs={{0,1},{1,0},{2,3},{3,2},{4,5},{5,4},{6,7},{7,6},{8,9},{9,8},{10,11... | collective-permute-start | bytes 110600 | tf_op jit(solution)/shard_map/ppermute | solution.py:234
  3.7 6.9 %collective-permute-start.3 = (f32[144,128]{1,0:T(8,128)S(1)}, f32[144,128]{1,0:T(8,128)S(1)}, u32[]{:S(2)}, u32[]{:S(2)}) collective-permute-start(f32[144,128]{1,0:T(8,128)S(1)} %pad_maximum_fusion.refs_0_), channel_id=1, source_target_pairs={{0,16},{1,0},{2,8},{3,24},{4,20},{5,4},{6,12},{7,28},{8,9},{9,1},{... | collective-permute-start | bytes 221192 | tf_op jit(solution)/shard_map/ppermute | solution.py:234
  7.6 4.5 %collective-permute-start.1 = (f32[144,128]{1,0:T(8,128)S(1)}, f32[144,128]{1,0:T(8,128)S(1)}, u32[]{:S(2)}, u32[]{:S(2)}) collective-permute-start(f32[144,128]{1,0:T(8,128)S(1)} %pad_maximum_fusion.refs_0_), channel_id=1, source_target_pairs={{0,24},{1,8},{2,16},{3,0},{4,28},{5,12},{6,20},{7,4},{8,17},{9,25}... | collective-permute-start | bytes 221192 | tf_op jit(solution)/shard_map/ppermute | solution.py:234
  9.5 4.4 %collective-permute-start.5 = (f32[144,128]{1,0:T(8,128)S(1)}, f32[144,128]{1,0:T(8,128)S(1)}, u32[]{:S(2)}, u32[]{:S(2)}) collective-permute-start(f32[144,128]{1,0:T(8,128)S(1)} %pad_maximum_fusion.refs_0_), channel_id=1, source_target_pairs={{0,2},{1,3},{2,0},{3,1},{4,6},{5,7},{6,4},{7,5},{8,10},{9,11},{10,... | collective-permute-start | bytes 221192 | tf_op jit(solution)/shard_map/ppermute | solution.py:234
  10.5 4.8 %collective-permute-start.4 = (f32[144,128]{1,0:T(8,128)S(1)}, f32[144,128]{1,0:T(8,128)S(1)}, u32[]{:S(2)}, u32[]{:S(2)}) collective-permute-start(f32[144,128]{1,0:T(8,128)S(1)} %collective-permute-done.3.refs_3_), channel_id=1, source_target_pairs={{0,4},{4,0},{8,12},{12,8},{16,20},{20,16},{24,28},{28,24},{1,5},{5... | collective-permute-start | bytes 221192 | tf_op jit(solution)/shard_map/ppermute | solution.py:238
  12.1 4.4 %collective-permute-start.2 = (f32[144,128]{1,0:T(8,128)S(1)}, f32[144,128]{1,0:T(8,128)S(1)}, u32[]{:S(2)}, u32[]{:S(2)}) collective-permute-start(f32[144,128]{1,0:T(8,128)S(1)} %collective-permute-done.1.refs_1_), channel_id=1, source_target_pairs={{0,4},{4,0},{8,12},{12,8},{16,20},{20,16},{24,28},{28,24},{1,5},{5... | collective-permute-start | bytes 221192 | tf_op jit(solution)/shard_map/ppermute | solution.py:238

commit v4 on v3

--- a/solution.py
+++ b/solution.py
@@ -14,13 +14,33 @@
 COLS = 2 * NFREQ
 LANES = 128
 VMEM_LIMIT = 16 << 20
-COLUMN_ROUNDS = (
-    ((3, 1, 2, 0), (2, 3, 0, 1), (3, 1, 0, 2), (2, 3, 1, 0)),
-    ((2, 0, 1, 3), (1, 0, 2, 3), (2, 0, 1, 3), (0, 1, 3, 2)),
-)
 SERIES = [(-1) ** n / math.factorial(2 * n) for n in range(8)]
 CONTRACT_LAST = (((1,), (1,)), ((), ()))
 CONTRACT_FIRST = (((0,), (0,)), ((), ()))
+
+
+TUNED_ROUNDS = (
+    (0, (
+        ((3, 1, 0, 2), (3, 1, 0, 2)),
+        ((2, 3, 1, 0), (2, 3, 1, 0)),
+        ((3, 1, 0, 2), (1, 3, 0, 2)),
+        ((0, 3, 2, 1), (2, 3, 1, 0)),
+    )),
+    (1, (
+        ((2, 0, 1, 3), (0, 2, 1, 3)),
+        ((0, 1, 2, 3), (1, 0, 3, 2)),
+        ((0, 2, 3, 1), (2, 0, 3, 1)),
+        ((2, 1, 0, 3), (1, 0, 2, 3)),
+    )),
+    (1, 0),
+    (0, (
+        ((2, 0, 1, 3), (2, 0, 1, 3)),
+        ((1, 0, 2, 3), (1, 0, 2, 3)),
+        ((0, 2, 1, 3), (2, 0, 1, 3)),
+        ((1, 2, 3, 0), (0, 1, 3, 2)),
+    )),
+    (None, 1),
+)
 
 
 def cosine_of(steps):
@@ -126,33 +146,25 @@
     return total
 
 
-def tiles_kernel(rounds, chips, ratio, scale, *refs):
-    own_ref = refs[0]
-    count = sum(1 if is_row else ratio for is_row, _ in rounds)
-    round_refs = list(refs[1 : 1 + count])
-    out_ref, left, right = refs[1 + count :]
-    tm = lax.axis_index("tm")
-    pt = lax.axis_index("pt")
+def tiles_kernel(origins, chips, ratio, scale, *refs):
+    blocks = refs[: len(origins)]
+    out_ref, left, right = refs[len(origins) :]
+    pt, tm = lax.axis_index("pt"), lax.axis_index("tm")
     device = pt * lax.axis_size("tm") + tm
     sub = lax.rem(pt, ratio)
     rows = left.shape[2]
     pairs = rows // COLS - 1
     points = LANES // 2
 
-    def put(dst, src, sender):
+    for (places, sources), ref in zip(origins, blocks, strict=True):
+        core = lookup([source % 2 for source in sources], device)
+        chip = lookup([source // 2 % chips for source in sources], device)
+        if places is None:
+            dst = left.at[chip]
+        else:
+            dst = right.at[lax.rem(sub + ratio - places, ratio), chip]
         for c in range(2):
-            dst[lax.rem(sender + c, 2)] = src[c * rows : (c + 1) * rows, :]
-
-    put(left.at[lax.div(tm, 2)], own_ref, lax.rem(tm, 2))
-    for is_row, targets in rounds:
-        sources = [targets.index(d) for d in range(len(targets))]
-        core = lookup([d % 2 for d in sources], device)
-        chip = lookup([d // 2 % chips for d in sources], device)
-        if is_row:
-            put(left.at[chip], round_refs.pop(0), core)
-        else:
-            for m in range(ratio):
-                put(right.at[lax.rem(sub + ratio - m, ratio), chip], round_refs.pop(0), core)
+            dst[lax.rem(core + c, 2)] = ref[c * rows : (c + 1) * rows, :]
 
     lane = lax.broadcasted_iota(jnp.int32, (pairs, LANES), 1)
     low_half = lane < points
@@ -210,18 +222,30 @@
         for core in range(2)
     ]
     number = {place: n for n, place in enumerate(devices)}
+
+    def column(places, groups):
+        targets = [
+            number[groups[g][s][2 * x + c], (s + places) % ratio, g // 2, g % 2] for g, s, x, c in devices
+        ]
+        return places, targets, None
+
+    def row(shift):
+        return None, [number[g, s, (x + shift) % chips, c] for g, s, x, c in devices], None
+
+    if (chips, ratio) == (2, 2):
+        return [
+            row(what) if places is None
+            else (places, None, what) if isinstance(what, int)
+            else column(places, what)
+            for places, what in TUNED_ROUNDS
+        ]
     rounds = []
     for m in range(chips):
-        if chips == len(COLUMN_ROUNDS):
-            groups = COLUMN_ROUNDS[m]
-        else:
-            order = [2 * ((x + m) % chips) + c for x in range(chips) for c in range(2)]
-            groups = [order] * cores
-        rounds.append((False, [
-            number[groups[g][2 * x + c], s, g // 2, g % 2] for g, s, x, c in devices
-        ]))
-    for m in range(1, chips):
-        rounds.append((True, [number[g, s, (x + m) % chips, c] for g, s, x, c in devices]))
+        order = [2 * ((x + m) % chips) + c for x in range(chips) for c in range(2)]
+        rounds.append(column(0, [[order] * ratio] * cores))
+    rounds += [row(shift) for shift in range(1, chips)]
+    for places in range(1, ratio):
+        rounds += [(places, None, m) for m in range(chips)]
     return rounds
 
 
@@ -229,31 +253,37 @@
     points, samples = signals.shape
     n_pt, n_tm = lax.axis_size("pt"), lax.axis_size("tm")
     ratio, chips = n_pt // n_tm, n_tm // 2
+    devices = range(n_pt * n_tm)
 
     def permute(value, targets):
         return lax.ppermute(value, ("pt", "tm"), list(enumerate(targets)))
 
-    def to_sub(value, m):
-        pairs = [(n, n // ratio * ratio + (n + m) % ratio) for n in range(n_pt)]
-        return lax.ppermute(value, "pt", pairs)
+    def moved(n, places):
+        sub = n // n_tm % ratio
+        return n + ((sub + places) % ratio - sub) * n_tm
 
     mine = project(signals, freq_bins)
-    other = permute(mine, [n ^ 1 for n in range(n_pt * n_tm)])
+    other = permute(mine, [n ^ 1 for n in devices])
     chip_block = jnp.concatenate([mine, other], axis=0)
-    rounds = plan_rounds(chips, ratio)
-    blocks = []
-    for is_row, targets in rounds:
-        blocks.append(permute(chip_block, targets))
-        if not is_row:
-            column = blocks[-1]
-            blocks += [to_sub(column, m) for m in range(1, ratio)]
-    rows = mine.shape[0]
+    blocks, origins = [], []
+    for places, targets, passed in plan_rounds(chips, ratio):
+        if passed is None:
+            blocks.append(permute(chip_block, targets))
+            origins.append((places, [targets.index(n) for n in devices]))
+        else:
+            blocks.append(permute(blocks[passed], [moved(n, places) for n in devices]))
+            before = origins[passed][1]
+            origins.append((places, [before[moved(n, -places)] for n in devices]))
+    blocks.append(chip_block)
+    origins.append((None, list(devices)))
+    blocks, origins = blocks[::-1], origins[::-1]
     segments = samples // HALF * n_tm - 1
     scale = 1.0 / (segments * 0.375 * SEGLEN)
+    rows = mine.shape[0]
     return pl.pallas_call(
-        functools.partial(tiles_kernel, rounds, chips, ratio, scale),
+        functools.partial(tiles_kernel, origins, chips, ratio, scale),
         out_shape=jax.ShapeDtypeStruct((2, NFREQ, points, ratio * points), jnp.float32),
-        in_specs=[pl.BlockSpec(memory_space=pltpu.VMEM)] * (1 + len(blocks)),
+        in_specs=[pl.BlockSpec(memory_space=pltpu.VMEM)] * len(blocks),
         out_specs=pl.BlockSpec(memory_space=pltpu.VMEM),
         scratch_shapes=[
             pltpu.VMEM((chips, 2, rows, LANES), jnp.float32),
@@ -261,7 +291,7 @@
         ],
         compiler_params=pltpu.CompilerParams(vmem_limit_bytes=VMEM_LIMIT),
         name="tiles",
-    )(chip_block, *blocks)
+    )(*blocks)
 
 
 def solution(mesh):

time: 17.8 us -> 16.7 us (0.938)
  starting transfers between devices: 10.3 us -> 9 us
  waiting for transfers between devices: 3.83 us -> 4.02 us
    ppermute x2 -> x0, starting transfers between devices: 2.91 us -> none  [to_sub(): return lax.ppermute(value, 'pt', pairs)]
    ppermute x4 -> x6, waiting for transfers between devices: 1.28 us -> 4.02 us  [permute(): return lax.ppermute(value, ('pt', 'tm'), list(enumerate(targets)))]
    ppermute x2 -> x0, waiting for transfers between devices: 2.55 us -> none  [to_sub(): return lax.ppermute(value, 'pt', pairs)]
    ppermute x4 -> x6, starting transfers between devices: 7.4 us -> 9 us  [permute(): return lax.ppermute(value, ('pt', 'tm'), list(enumerate(targets)))]
where the time goes in v4:
time: 16.7 us; the launch traced here: 16.5 us
  starting transfers between devices  9 us (54%)
  waiting for transfers between devices  4.02 us (24%)
  Pallas kernels  3.47 us (21%)
    ppermute x6, starting transfers between devices, permute(): return lax.ppermute(value, ('pt', 'tm'), list(enumerate(targets)))  9 us
    ppermute x6, waiting for transfers between devices, permute(): return lax.ppermute(value, ('pt', 'tm'), list(enumerate(targets)))  4.02 us
    pallas_call x1, Pallas kernels, project(): pl.pallas_call(project_kernel, out_shape=jax.ShapeDtypeStruct(((pairs + 1...  2.26 us
    pallas_call x1, Pallas kernels, body(): pl.pallas_call(functools.partial(tiles_kernel, origins, chips, ratio, sca...  1.21 us
  transfers between devices with their start and end apart: 6, of which 4 were waited for; matrix products, arithmetic and copies ran while one was open for 0% of the time, Pallas kernels for 0%

profile of v4, /device:TPU:0, one launch (start us, length us, event | category | flops | bytes accessed | tf_op | source)
XLA Modules:
  0.0 16.5 jit_solution(3670504785779020161)
XLA Ops:
  0.0 2.3 %project.1 = f32[72,128]{1,0:T(8,128)S(1)} custom-call(s32[4]{0:T(128)} %bins_hbm.1, f32[64,8192]{1,0:T(8,128)} %signals_ref.1), custom_call_target="tpu_custom_call" | custom-call | tf_op jit(solution)/shard_map/project/pallas_call | solution.py:120
  2.3 0.5 %collective-permute-start = (f32[72,128]{1,0:T(8,128)S(1)}, f32[72,128]{1,0:T(8,128)S(1)}, u32[]{:S(2)}, u32[]{:S(2)}) collective-permute-start(f32[72,128]{1,0:T(8,128)S(1)} %project.1), channel_id=1, source_target_pairs={{0,1},{1,0},{2,3},{3,2},{4,5},{5,4},{6,7},{7,6},{8,9},{9,8},{10,11... | collective-permute-start | bytes 110600 | tf_op jit(solution)/shard_map/ppermute | solution.py:259
  2.8 0.9 %collective-permute-done = f32[72,128]{1,0:T(8,128)S(1)} collective-permute-done((f32[72,128]{1,0:T(8,128)S(1)}, f32[72,128]{1,0:T(8,128)S(1)}, u32[]{:S(2)}, u32[]{:S(2)}) %collective-permute-start) | collective-permute-done | bytes 36896 | tf_op jit(solution)/shard_map/ppermute | solution.py:259
  3.7 4.9 %collective-permute-start.3 = (f32[144,128]{1,0:T(8,128)S(1)}, f32[144,128]{1,0:T(8,128)S(1)}, u32[]{:S(2)}, u32[]{:S(2)}) collective-permute-start(f32[144,128]{1,0:T(8,128)S(1)} %pad_maximum_fusion.refs_0_), channel_id=1, source_target_pairs={{0,24},{1,8},{2,0},{3,16},{4,28},{5,12},{6,4},{7,20},{8,17},{9,25}... | collective-permute-start | bytes 221192 | tf_op jit(solution)/shard_map/ppermute | solution.py:259
  8.6 1.3 %collective-permute-start.5 = (f32[144,128]{1,0:T(8,128)S(1)}, f32[144,128]{1,0:T(8,128)S(1)}, u32[]{:S(2)}, u32[]{:S(2)}) collective-permute-start(f32[144,128]{1,0:T(8,128)S(1)} %pad_maximum_fusion.refs_0_), channel_id=1, source_target_pairs={{0,20},{1,4},{2,12},{3,28},{4,0},{5,16},{6,8},{7,24},{8,5},{9,13},... | collective-permute-start | bytes 221192 | tf_op jit(solution)/shard_map/ppermute | solution.py:259
  9.9 0.4 %collective-permute-start.2 = (f32[144,128]{1,0:T(8,128)S(1)}, f32[144,128]{1,0:T(8,128)S(1)}, u32[]{:S(2)}, u32[]{:S(2)}) collective-permute-start(f32[144,128]{1,0:T(8,128)S(1)} %pad_maximum_fusion.refs_0_), channel_id=1, source_target_pairs={{0,16},{1,0},{2,8},{3,24},{4,20},{5,4},{6,12},{7,28},{8,9},{9,1},{... | collective-permute-start | bytes 221192 | tf_op jit(solution)/shard_map/ppermute | solution.py:259
  10.3 0.4 %collective-permute-start.1 = (f32[144,128]{1,0:T(8,128)S(1)}, f32[144,128]{1,0:T(8,128)S(1)}, u32[]{:S(2)}, u32[]{:S(2)}) collective-permute-start(f32[144,128]{1,0:T(8,128)S(1)} %pad_maximum_fusion.refs_0_), channel_id=1, source_target_pairs={{0,2},{1,3},{2,0},{3,1},{4,6},{5,7},{6,4},{7,5},{8,10},{9,11},{10,... | collective-permute-start | bytes 221192 | tf_op jit(solution)/shard_map/ppermute | solution.py:259
  10.7 0.0 collective-permute-done.3.refs_5_
  10.7 1.4 %collective-permute-start.4 = (f32[144,128]{1,0:T(8,128)S(1)}, f32[144,128]{1,0:T(8,128)S(1)}, u32[]{:S(2)}, u32[]{:S(2)}) collective-permute-start(f32[144,128]{1,0:T(8,128)S(1)} %collective-permute-done.3.refs_5_), channel_id=1, source_target_pairs={{0,4},{1,5},{2,6},{3,7},{4,0},{5,1},{6,2},{7,3},{8,12},{9,13},{10,... | collective-permute-start | bytes 221192 | tf_op jit(solution)/shard_map/ppermute | solution.py:259
  12.1 0.8 %collective-permute-done.5.refs_4_ = f32[144,128]{1,0:T(8,128)S(1)} collective-permute-done((f32[144,128]{1,0:T(8,128)S(1)}, f32[144,128]{1,0:T(8,128)S(1)}, u32[]{:S(2)}, u32[]{:S(2)}) %collective-permute-start.5) | collective-permute-done | bytes 73760 | tf_op jit(solution)/shard_map/ppermute | solution.py:259
  13.0 0.0 collective-permute-done.2.refs_2_
  13.0 2.1 %collective-permute-done.1.refs_1_ = f32[144,128]{1,0:T(8,128)S(1)} collective-permute-done((f32[144,128]{1,0:T(8,128)S(1)}, f32[144,128]{1,0:T(8,128)S(1)}, u32[]{:S(2)}, u32[]{:S(2)}) %collective-permute-start.1) | collective-permute-done | bytes 73760 | tf_op jit(solution)/shard_map/ppermute | solution.py:259
  15.1 0.2 %collective-permute-done.4.refs_3_ = f32[144,128]{1,0:T(8,128)S(1)} collective-permute-done((f32[144,128]{1,0:T(8,128)S(1)}, f32[144,128]{1,0:T(8,128)S(1)}, u32[]{:S(2)}, u32[]{:S(2)}) %collective-permute-start.4) | collective-permute-done | bytes 73760 | tf_op jit(solution)/shard_map/ppermute | solution.py:259
  15.3 1.2 %tiles.1 = f32[2,4,64,128]{3,2,1,0:T(8,128)} custom-call(f32[144,128]{1,0:T(8,128)S(1)} %pad_maximum_fusion.refs_0_, f32[144,128]{1,0:T(8,128)S(1)} %collective-permute-done.1.refs_1_, f32[144,128]{1,0:T(8,128)S(1)} %collective-permute-done.2.refs_2_, f32[144,128]{1,0:T(8,128)S(1)} %collective-permute-done.4.refs_3_, ...), custom_call_target="tpu_custom_call" | custom-call | tf_op jit(solution)/shard_map/tiles/pallas_call | solution.py:283
  (1 shorter events, 0.0 us)
Async XLA Ops:
  2.3 1.4 %collective-permute-start = (f32[72,128]{1,0:T(8,128)S(1)}, f32[72,128]{1,0:T(8,128)S(1)}, u32[]{:S(2)}, u32[]{:S(2)}) collective-permute-start(f32[72,128]{1,0:T(8,128)S(1)} %project.1), channel_id=1, source_target_pairs={{0,1},{1,0},{2,3},{3,2},{4,5},{5,4},{6,7},{7,6},{8,9},{9,8},{10,11... | collective-permute-start | bytes 110600 | tf_op jit(solution)/shard_map/ppermute | solution.py:259
  3.7 7.1 %collective-permute-start.3 = (f32[144,128]{1,0:T(8,128)S(1)}, f32[144,128]{1,0:T(8,128)S(1)}, u32[]{:S(2)}, u32[]{:S(2)}) collective-permute-start(f32[144,128]{1,0:T(8,128)S(1)} %pad_maximum_fusion.refs_0_), channel_id=1, source_target_pairs={{0,24},{1,8},{2,0},{3,16},{4,28},{5,12},{6,4},{7,20},{8,17},{9,25}... | collective-permute-start | bytes 221192 | tf_op jit(solution)/shard_map/ppermute | solution.py:259
  8.6 4.4 %collective-permute-start.5 = (f32[144,128]{1,0:T(8,128)S(1)}, f32[144,128]{1,0:T(8,128)S(1)}, u32[]{:S(2)}, u32[]{:S(2)}) collective-permute-start(f32[144,128]{1,0:T(8,128)S(1)} %pad_maximum_fusion.refs_0_), channel_id=1, source_target_pairs={{0,20},{1,4},{2,12},{3,28},{4,0},{5,16},{6,8},{7,24},{8,5},{9,13},... | collective-permute-start | bytes 221192 | tf_op jit(solution)/shard_map/ppermute | solution.py:259
  9.9 3.0 %collective-permute-start.2 = (f32[144,128]{1,0:T(8,128)S(1)}, f32[144,128]{1,0:T(8,128)S(1)}, u32[]{:S(2)}, u32[]{:S(2)}) collective-permute-start(f32[144,128]{1,0:T(8,128)S(1)} %pad_maximum_fusion.refs_0_), channel_id=1, source_target_pairs={{0,16},{1,0},{2,8},{3,24},{4,20},{5,4},{6,12},{7,28},{8,9},{9,1},{... | collective-permute-start | bytes 221192 | tf_op jit(solution)/shard_map/ppermute | solution.py:259
  10.3 4.7 %collective-permute-start.1 = (f32[144,128]{1,0:T(8,128)S(1)}, f32[144,128]{1,0:T(8,128)S(1)}, u32[]{:S(2)}, u32[]{:S(2)}) collective-permute-start(f32[144,128]{1,0:T(8,128)S(1)} %pad_maximum_fusion.refs_0_), channel_id=1, source_target_pairs={{0,2},{1,3},{2,0},{3,1},{4,6},{5,7},{6,4},{7,5},{8,10},{9,11},{10,... | collective-permute-start | bytes 221192 | tf_op jit(solution)/shard_map/ppermute | solution.py:259
  10.7 4.6 %collective-permute-start.4 = (f32[144,128]{1,0:T(8,128)S(1)}, f32[144,128]{1,0:T(8,128)S(1)}, u32[]{:S(2)}, u32[]{:S(2)}) collective-permute-start(f32[144,128]{1,0:T(8,128)S(1)} %collective-permute-done.3.refs_5_), channel_id=1, source_target_pairs={{0,4},{1,5},{2,6},{3,7},{4,0},{5,1},{6,2},{7,3},{8,12},{9,13},{10,... | collective-permute-start | bytes 221192 | tf_op jit(solution)/shard_map/ppermute | solution.py:259

commit v5 on v4

--- a/solution.py
+++ b/solution.py
@@ -146,67 +146,141 @@
     return total
 
 
-def tiles_kernel(origins, chips, ratio, scale, *refs):
-    blocks = refs[: len(origins)]
-    out_ref, left, right = refs[len(origins) :]
+def join(low, high):
+    points = LANES // 2
+    is_low = lax.broadcasted_iota(jnp.int32, low.shape, 1) < points
+    return (
+        jnp.where(is_low, low, pltpu.roll(high, points, 1)),
+        jnp.where(is_low, pltpu.roll(low, points, 1), high),
+    )
+
+
+def place_of(sources, chips, device):
+    chip = lookup([source // 2 % chips for source in sources], device)
+    return chip, lookup([source % 2 for source in sources], device)
+
+
+def put(dst, src, sender):
+    rows = src.shape[0] // 2
+    for c in range(2):
+        dst[lax.rem(sender + c, 2)] = src[c * rows : (c + 1) * rows, :]
+
+
+def this_device():
     pt, tm = lax.axis_index("pt"), lax.axis_index("tm")
-    device = pt * lax.axis_size("tm") + tm
+    return pt * lax.axis_size("tm") + tm, pt, tm
+
+
+def prepare_kernel(rows_from, columns_from, chips, ratio, *refs):
+    own_ref = refs[0]
+    column_refs = refs[1 : len(columns_from)]
+    row_refs = refs[len(columns_from) : len(rows_from) + len(columns_from)]
+    lhs_high_ref, lhs_low_ref, rhs_ref, tail_ref, left, right = refs[len(rows_from) + len(columns_from) :]
+    device, pt, tm = this_device()
     sub = lax.rem(pt, ratio)
-    rows = left.shape[2]
-    pairs = rows // COLS - 1
+    times = 2 * chips
+    pairs = left.shape[2] // COLS - 1
     points = LANES // 2
 
-    for (places, sources), ref in zip(origins, blocks, strict=True):
-        core = lookup([source % 2 for source in sources], device)
-        chip = lookup([source // 2 % chips for source in sources], device)
-        if places is None:
-            dst = left.at[chip]
-        else:
-            dst = right.at[lax.rem(sub + ratio - places, ratio), chip]
-        for c in range(2):
-            dst[lax.rem(core + c, 2)] = ref[c * rows : (c + 1) * rows, :]
-
-    lane = lax.broadcasted_iota(jnp.int32, (pairs, LANES), 1)
-    low_half = lane < points
-    last_row = (pairs - 1) * COLS
-    low_lanes = lax.broadcasted_iota(jnp.int32, (COLS, LANES), 1) < points
-
-    def finish(at):
-        for t in range(2 * chips):
-            here = at(t)
-            value = here[last_row : last_row + COLS, :]
-            if t + 1 < 2 * chips:
-                extra = pltpu.roll(at(t + 1)[pairs * COLS :, :], points, 1)
-                value = jnp.where(low_lanes, value, value + extra)
+    put(left.at[lax.div(tm, 2)], own_ref, lax.rem(tm, 2))
+    for sources, ref in zip(rows_from, row_refs, strict=True):
+        chip, core = place_of(sources, chips, device)
+        put(left.at[chip], ref, core)
+    for (m, sources), ref in zip(columns_from[:-1], column_refs, strict=True):
+        chip, core = place_of(sources, chips, device)
+        put(right.at[lax.rem(sub + ratio - m, ratio), chip], ref, core)
+    m, sources = columns_from[-1]
+    last_sub = lax.rem(sub + ratio - m, ratio)
+    last_chip, _ = place_of(sources, chips, device)
+
+    ends = pl.ds((pairs - 1) * COLS, COLS)
+    heads = pl.ds(pairs * COLS, COLS)
+    is_low = lax.broadcasted_iota(jnp.int32, (COLS, LANES), 1) < points
+
+    def finish(at, missing):
+        for t in range(times):
+            value = at(t)[ends, :]
+            if t + 1 < times:
+                extra = pltpu.roll(at(t + 1)[heads, :], points, 1)
+                if t % 2:
+                    extra = jnp.where(missing(t // 2 + 1), 0.0, extra)
+                at(t)[ends, :] = jnp.where(is_low, value, value + extra)
             else:
-                value = jnp.where(low_lanes, value, 0.0)
-            here[last_row : last_row + COLS, :] = value
-
-    finish(lambda t: left.at[t // 2, t % 2])
+                at(t)[ends, :] = jnp.where(is_low, value, 0.0)
+
+    after = right.at[last_sub, jnp.minimum(last_chip + 1, chips - 1), 0]
+    tail_ref[...] = pltpu.roll(after[heads, :], points, 1)
+    finish(lambda t: left.at[t // 2, t % 2], lambda chip: False)
     for b in range(ratio):
-        finish(lambda t, b=b: right.at[b, t // 2, t % 2])
-
-    def join(low, high):
-        return (
-            jnp.where(low_half, low, pltpu.roll(high, points, 1)),
-            jnp.where(low_half, pltpu.roll(low, points, 1), high),
+        finish(
+            lambda t, b=b: right.at[b, t // 2, t % 2],
+            lambda chip, b=b: jnp.logical_and(last_sub == b, last_chip == chip),
         )
 
     for f in range(NFREQ):
         lhs, rhs = [[], []], [[], []]
-        for t in range(2 * chips):
-            real, imag = (left.at[t // 2, t % 2][pl.ds(part * NFREQ + f, pairs, stride=COLS), :] for part in range(2))
+        for t in range(times):
+            real, imag = (
+                left.at[t // 2, t % 2][pl.ds(part * NFREQ + f, pairs, stride=COLS), :]
+                for part in range(2)
+            )
             lhs[0] += join(real, imag)
             lhs[1] += join(imag, -real)
             for part in range(2):
                 pick = pl.ds(part * NFREQ + f, pairs, stride=COLS)
-                rhs[part] += join(*(right.at[b, t // 2, t % 2][pick, :] for b in range(2)))
-        lhs_high, lhs_low = split(jnp.concatenate(lhs[0] + lhs[1], axis=0))
-        rhs_high, rhs_low = split(jnp.concatenate(rhs[0] + rhs[1], axis=0))
-        dot = functools.partial(
-            lax.dot_general, dimension_numbers=CONTRACT_FIRST, preferred_element_type=jnp.float32
-        )
-        tile = dot(lhs_high, rhs_high) + (dot(lhs_high, rhs_low) + dot(lhs_low, rhs_high))
+                rhs[part] += join(*(right.at[b, t // 2, t % 2][pick, :] for b in range(ratio)))
+        lhs_high_ref[f], lhs_low_ref[f] = split(jnp.concatenate(lhs[0] + lhs[1], axis=0).T)
+        rhs_ref[f] = jnp.concatenate(rhs[0] + rhs[1], axis=0)
+
+
+def tiles_kernel(
+    last_from, chips, ratio, scale, lhs_high_ref, lhs_low_ref, rhs_ref, tail_ref, last_ref, out_ref, last
+):
+    device, pt, _ = this_device()
+    times = 2 * chips
+    pairs = last.shape[1] // COLS - 1
+    points = LANES // 2
+    m, sources = last_from
+    is_first = lax.rem(lax.rem(pt, ratio) + ratio - m, ratio) == 0
+    last_chip, core = place_of(sources, chips, device)
+    put(last, last_ref, core)
+
+    ends = pl.ds((pairs - 1) * COLS, COLS)
+    heads = pl.ds(pairs * COLS, COLS)
+    is_low = lax.broadcasted_iota(jnp.int32, (COLS, LANES), 1) < points
+    value = last[0, ends, :]
+    last[0, ends, :] = jnp.where(is_low, value, value + pltpu.roll(last[1, heads, :], points, 1))
+    value = last[1, ends, :]
+    ended = jnp.where(last_chip == chips - 1, 0.0, value + tail_ref[...])
+    last[1, ends, :] = jnp.where(is_low, value, ended)
+
+    lane = lax.broadcasted_iota(jnp.int32, (pairs, LANES), 1)
+    mine = jnp.where(is_first, lane, LANES - 1 - lane) < points
+    from_here = [jnp.logical_and(mine, last_chip == chip) for chip in range(chips)]
+    end_row = lax.broadcasted_iota(jnp.int32, (pairs, LANES), 0) == pairs - 1
+    head = last[0, heads, :]
+    head = jnp.where(is_first, head, pltpu.roll(head, points, 1))
+    dot = functools.partial(jnp.dot, preferred_element_type=jnp.float32)
+    for f in range(NFREQ):
+        rhs = []
+        for part in range(2):
+            column = part * NFREQ + f
+            new = []
+            for c in range(2):
+                picked = last[c, pl.ds(column, pairs, stride=COLS), :]
+                turned = pltpu.roll(picked, points, 1)
+                new.append((jnp.where(is_first, picked, turned), jnp.where(is_first, turned, picked)))
+            for t in range(times):
+                for h in range(2):
+                    start = ((part * times + t) * 2 + h) * pairs
+                    value = rhs_ref[f, start : start + pairs, :]
+                    if h == 1 and t % 2 == 1 and t + 1 < times:
+                        here = jnp.logical_and(end_row, from_here[t // 2 + 1])
+                        value = value + jnp.where(here, head[column : column + 1, :], 0.0)
+                    rhs.append(jnp.where(from_here[t // 2], new[t % 2][h], value))
+        rhs_high, rhs_low = split(jnp.concatenate(rhs, axis=0))
+        high, low = lhs_high_ref[f], lhs_low_ref[f]
+        tile = dot(high, rhs_high) + (dot(high, rhs_low) + dot(low, rhs_high))
         tile = tile * scale
         out_ref[0, f] = tile[:points]
         out_ref[1, f] = tile[points:]
@@ -266,7 +340,8 @@
     other = permute(mine, [n ^ 1 for n in devices])
     chip_block = jnp.concatenate([mine, other], axis=0)
     blocks, origins = [], []
-    for places, targets, passed in plan_rounds(chips, ratio):
+    plan = plan_rounds(chips, ratio)
+    for places, targets, passed in plan:
         if passed is None:
             blocks.append(permute(chip_block, targets))
             origins.append((places, [targets.index(n) for n in devices]))
@@ -274,24 +349,45 @@
             blocks.append(permute(blocks[passed], [moved(n, places) for n in devices]))
             before = origins[passed][1]
             origins.append((places, [before[moved(n, -places)] for n in devices]))
-    blocks.append(chip_block)
-    origins.append((None, list(devices)))
-    blocks, origins = blocks[::-1], origins[::-1]
+    *_, last = (n for n, (places, targets, _) in enumerate(plan) if places is not None and targets is None)
+    order = [n for n in range(len(plan)) if n != last] + [last]
+    rows = [blocks[n] for n in order if origins[n][0] is None]
+    rows_from = [origins[n][1] for n in order if origins[n][0] is None]
+    columns = [blocks[n] for n in order if origins[n][0] is not None]
+    columns_from = [origins[n] for n in order if origins[n][0] is not None]
+    depth = mine.shape[0] - COLS
+    depth = depth // COLS * 2 * 2 * n_tm
     segments = samples // HALF * n_tm - 1
-    scale = 1.0 / (segments * 0.375 * SEGLEN)
-    rows = mine.shape[0]
+    params = pltpu.CompilerParams(vmem_limit_bytes=VMEM_LIMIT)
+    in_vmem = pl.BlockSpec(memory_space=pltpu.VMEM)
+    block = (2, mine.shape[0], LANES)
+    side = jax.ShapeDtypeStruct((NFREQ, LANES, depth), jnp.bfloat16)
+    *sides, tail = pl.pallas_call(
+        functools.partial(prepare_kernel, rows_from, columns_from, chips, ratio),
+        out_shape=[
+            side,
+            side,
+            jax.ShapeDtypeStruct((NFREQ, depth, LANES), jnp.float32),
+            jax.ShapeDtypeStruct((COLS, LANES), jnp.float32),
+        ],
+        in_specs=[in_vmem] * (len(rows) + len(columns)),
+        out_specs=[in_vmem] * 4,
+        scratch_shapes=[
+            pltpu.VMEM((chips, *block), jnp.float32),
+            pltpu.VMEM((ratio, chips, *block), jnp.float32),
+        ],
+        compiler_params=params,
+        name="prepare",
+    )(chip_block, *columns[:-1], *rows)
     return pl.pallas_call(
-        functools.partial(tiles_kernel, origins, chips, ratio, scale),
+        functools.partial(tiles_kernel, columns_from[-1], chips, ratio, 1.0 / (segments * 0.375 * SEGLEN)),
         out_shape=jax.ShapeDtypeStruct((2, NFREQ, points, ratio * points), jnp.float32),
-        in_specs=[pl.BlockSpec(memory_space=pltpu.VMEM)] * len(blocks),
-        out_specs=pl.BlockSpec(memory_space=pltpu.VMEM),
-        scratch_shapes=[
-            pltpu.VMEM((chips, 2, rows, LANES), jnp.float32),
-            pltpu.VMEM((ratio, chips, 2, rows, LANES), jnp.float32),
-        ],
-        compiler_params=pltpu.CompilerParams(vmem_limit_bytes=VMEM_LIMIT),
+        in_specs=[in_vmem] * 5,
+        out_specs=in_vmem,
+        scratch_shapes=[pltpu.VMEM(block, jnp.float32)],
+        compiler_params=params,
         name="tiles",
-    )(*blocks)
+    )(*sides, tail, columns[-1])
 
 
 def solution(mesh):

time: 16.7 us -> 17 us (1.018)
  the two profiles are of different devices: /device:TPU:0 before, /device:TPU:25 now
where the time goes in v5:
time: 17 us; the launch traced here: 16.9 us
  starting transfers between devices  7.52 us (44%)
  waiting for transfers between devices  5.54 us (33%)
  Pallas kernels  3.78 us (22%)
    ppermute x6, starting transfers between devices, permute(): return lax.ppermute(value, ('pt', 'tm'), list(enumerate(targets)))  7.52 us
    ppermute x6, waiting for transfers between devices, permute(): return lax.ppermute(value, ('pt', 'tm'), list(enumerate(targets)))  5.54 us
    pallas_call x1, Pallas kernels, project(): pl.pallas_call(project_kernel, out_shape=jax.ShapeDtypeStruct(((pairs + 1...  2.26 us
    pallas_call x1, Pallas kernels, body(): pl.pallas_call(functools.partial(tiles_kernel, columns_from[-1], chips, r...  1.15 us
    pallas_call x1, Pallas kernels, body(): pl.pallas_call(functools.partial(prepare_kernel, rows_from, columns_from,...  0.38 us
  transfers between devices with their start and end apart: 6, of which 4 were waited for; matrix products, arithmetic and copies ran while one was open for 0% of the time, Pallas kernels for 2%

profile of v5, /device:TPU:25, one launch (start us, length us, event | category | flops | bytes accessed | tf_op | source)
XLA Modules:
  0.0 16.9 jit_solution(9140648438192170325)
XLA Ops:
  0.0 2.3 %project.1 = f32[72,128]{1,0:T(8,128)S(1)} custom-call(s32[4]{0:T(128)} %bins_hbm.1, f32[64,8192]{1,0:T(8,128)} %signals_ref.1), custom_call_target="tpu_custom_call" | custom-call | tf_op jit(solution)/shard_map/project/pallas_call | solution.py:120
  2.3 0.7 %collective-permute-start = (f32[72,128]{1,0:T(8,128)S(1)}, f32[72,128]{1,0:T(8,128)S(1)}, u32[]{:S(2)}, u32[]{:S(2)}) collective-permute-start(f32[72,128]{1,0:T(8,128)S(1)} %project.1), channel_id=1, source_target_pairs={{0,1},{1,0},{2,3},{3,2},{4,5},{5,4},{6,7},{7,6},{8,9},{9,8},{10,11... | collective-permute-start | bytes 110600 | tf_op jit(solution)/shard_map/ppermute | solution.py:333
  3.0 0.9 %collective-permute-done = f32[72,128]{1,0:T(8,128)S(1)} collective-permute-done((f32[72,128]{1,0:T(8,128)S(1)}, f32[72,128]{1,0:T(8,128)S(1)}, u32[]{:S(2)}, u32[]{:S(2)}) %collective-permute-start) | collective-permute-done | bytes 36896 | tf_op jit(solution)/shard_map/ppermute | solution.py:333
  3.9 1.2 %collective-permute-start.1 = (f32[144,128]{1,0:T(8,128)S(1)}, f32[144,128]{1,0:T(8,128)S(1)}, u32[]{:S(2)}, u32[]{:S(2)}) collective-permute-start(f32[144,128]{1,0:T(8,128)S(1)} %pad_maximum_fusion.refs_0_), channel_id=1, source_target_pairs={{0,24},{1,8},{2,0},{3,16},{4,28},{5,12},{6,4},{7,20},{8,17},{9,25}... | collective-permute-start | bytes 221192 | tf_op jit(solution)/shard_map/ppermute | solution.py:333
  5.1 0.9 %collective-permute-start.2 = (f32[144,128]{1,0:T(8,128)S(1)}, f32[144,128]{1,0:T(8,128)S(1)}, u32[]{:S(2)}, u32[]{:S(2)}) collective-permute-start(f32[144,128]{1,0:T(8,128)S(1)} %pad_maximum_fusion.refs_0_), channel_id=1, source_target_pairs={{0,20},{1,4},{2,12},{3,28},{4,0},{5,16},{6,8},{7,24},{8,5},{9,13},... | collective-permute-start | bytes 221192 | tf_op jit(solution)/shard_map/ppermute | solution.py:333
  6.0 0.7 %collective-permute-start.3 = (f32[144,128]{1,0:T(8,128)S(1)}, f32[144,128]{1,0:T(8,128)S(1)}, u32[]{:S(2)}, u32[]{:S(2)}) collective-permute-start(f32[144,128]{1,0:T(8,128)S(1)} %pad_maximum_fusion.refs_0_), channel_id=1, source_target_pairs={{0,16},{1,0},{2,8},{3,24},{4,20},{5,4},{6,12},{7,28},{8,9},{9,1},{... | collective-permute-start | bytes 221192 | tf_op jit(solution)/shard_map/ppermute | solution.py:333
  6.6 4.0 %collective-permute-start.4 = (f32[144,128]{1,0:T(8,128)S(1)}, f32[144,128]{1,0:T(8,128)S(1)}, u32[]{:S(2)}, u32[]{:S(2)}) collective-permute-start(f32[144,128]{1,0:T(8,128)S(1)} %pad_maximum_fusion.refs_0_), channel_id=1, source_target_pairs={{0,2},{1,3},{2,0},{3,1},{4,6},{5,7},{6,4},{7,5},{8,10},{9,11},{10,... | collective-permute-start | bytes 221192 | tf_op jit(solution)/shard_map/ppermute | solution.py:333
  10.7 0.0 collective-permute-done.1.refs_1_
  10.7 0.0 collective-permute-start.5
  10.7 2.0 %collective-permute-done.2.refs_2_ = f32[144,128]{1,0:T(8,128)S(1)} collective-permute-done((f32[144,128]{1,0:T(8,128)S(1)}, f32[144,128]{1,0:T(8,128)S(1)}, u32[]{:S(2)}, u32[]{:S(2)}) %collective-permute-start.2) | collective-permute-done | bytes 73760 | tf_op jit(solution)/shard_map/ppermute | solution.py:333
  12.6 1.6 %collective-permute-done.3.refs_3_ = f32[144,128]{1,0:T(8,128)S(1)} collective-permute-done((f32[144,128]{1,0:T(8,128)S(1)}, f32[144,128]{1,0:T(8,128)S(1)}, u32[]{:S(2)}, u32[]{:S(2)}) %collective-permute-start.3) | collective-permute-done | bytes 73760 | tf_op jit(solution)/shard_map/ppermute | solution.py:333
  14.2 1.1 %collective-permute-done.4.refs_4_ = f32[144,128]{1,0:T(8,128)S(1)} collective-permute-done((f32[144,128]{1,0:T(8,128)S(1)}, f32[144,128]{1,0:T(8,128)S(1)}, u32[]{:S(2)}, u32[]{:S(2)}) %collective-permute-start.4) | collective-permute-done | bytes 73760 | tf_op jit(solution)/shard_map/ppermute | solution.py:333
  15.3 0.4 %prepare.1 = (bf16[4,128,128]{2,1,0:T(8,128)(2,1)S(1)}, bf16[4,128,128]{2,1,0:T(8,128)(2,1)S(1)}, f32[4,128,128]{2,1,0:T(8,128)S(1)}, f32[8,128]{1,0:T(8,128)S(1)}) custom-call(f32[144,128]{1,0:T(8,128)S(1)} %pad_maximum_fusion.refs_0_, f32[144,128]{1,0:T(8,128)S(1)} %collective-permute-done.1.refs_1_, f32[144,128]{1,0:T(8,128)S(1)} %collective-permute-done.2.refs_2_, ...), custom_call_target="tpu_custom_call" | custom-call | tf_op jit(solution)/shard_map/prepare/pallas_call | solution.py:365
  15.7 0.0 collective-permute-done.5.last_ref
  15.7 1.1 %tiles.1 = f32[2,4,64,128]{3,2,1,0:T(8,128)} custom-call(bf16[4,128,128]{2,1,0:T(8,128)(2,1)S(1)} %get-tuple-element.9.lhs_high_ref, bf16[4,128,128]{2,1,0:T(8,128)(2,1)S(1)} %get-tuple-element.10.lhs_low_ref, f32[4,128,128]{2,1,0:T(8,128)S(1)} %get-tuple-element.11.rhs_ref, f32[8,128]{1,0:T(8,128)S(1)} %get-tuple-element.12.tail_ref, ...), custom_call_target="tpu_custom_call" | custom-call | tf_op jit(solution)/shard_map/tiles/pallas_call | solution.py:382
  (1 shorter events, 0.0 us)
Async XLA Ops:
  2.3 1.6 %collective-permute-start = (f32[72,128]{1,0:T(8,128)S(1)}, f32[72,128]{1,0:T(8,128)S(1)}, u32[]{:S(2)}, u32[]{:S(2)}) collective-permute-start(f32[72,128]{1,0:T(8,128)S(1)} %project.1), channel_id=1, source_target_pairs={{0,1},{1,0},{2,3},{3,2},{4,5},{5,4},{6,7},{7,6},{8,9},{9,8},{10,11... | collective-permute-start | bytes 110600 | tf_op jit(solution)/shard_map/ppermute | solution.py:333
  3.9 6.8 %collective-permute-start.1 = (f32[144,128]{1,0:T(8,128)S(1)}, f32[144,128]{1,0:T(8,128)S(1)}, u32[]{:S(2)}, u32[]{:S(2)}) collective-permute-start(f32[144,128]{1,0:T(8,128)S(1)} %pad_maximum_fusion.refs_0_), channel_id=1, source_target_pairs={{0,24},{1,8},{2,0},{3,16},{4,28},{5,12},{6,4},{7,20},{8,17},{9,25}... | collective-permute-start | bytes 221192 | tf_op jit(solution)/shard_map/ppermute | solution.py:333
  5.1 7.5 %collective-permute-start.2 = (f32[144,128]{1,0:T(8,128)S(1)}, f32[144,128]{1,0:T(8,128)S(1)}, u32[]{:S(2)}, u32[]{:S(2)}) collective-permute-start(f32[144,128]{1,0:T(8,128)S(1)} %pad_maximum_fusion.refs_0_), channel_id=1, source_target_pairs={{0,20},{1,4},{2,12},{3,28},{4,0},{5,16},{6,8},{7,24},{8,5},{9,13},... | collective-permute-start | bytes 221192 | tf_op jit(solution)/shard_map/ppermute | solution.py:333
  6.0 8.3 %collective-permute-start.3 = (f32[144,128]{1,0:T(8,128)S(1)}, f32[144,128]{1,0:T(8,128)S(1)}, u32[]{:S(2)}, u32[]{:S(2)}) collective-permute-start(f32[144,128]{1,0:T(8,128)S(1)} %pad_maximum_fusion.refs_0_), channel_id=1, source_target_pairs={{0,16},{1,0},{2,8},{3,24},{4,20},{5,4},{6,12},{7,28},{8,9},{9,1},{... | collective-permute-start | bytes 221192 | tf_op jit(solution)/shard_map/ppermute | solution.py:333
  6.6 8.7 %collective-permute-start.4 = (f32[144,128]{1,0:T(8,128)S(1)}, f32[144,128]{1,0:T(8,128)S(1)}, u32[]{:S(2)}, u32[]{:S(2)}) collective-permute-start(f32[144,128]{1,0:T(8,128)S(1)} %pad_maximum_fusion.refs_0_), channel_id=1, source_target_pairs={{0,2},{1,3},{2,0},{3,1},{4,6},{5,7},{6,4},{7,5},{8,10},{9,11},{10,... | collective-permute-start | bytes 221192 | tf_op jit(solution)/shard_map/ppermute | solution.py:333
  10.7 5.1 %collective-permute-start.5 = (f32[144,128]{1,0:T(8,128)S(1)}, f32[144,128]{1,0:T(8,128)S(1)}, u32[]{:S(2)}, u32[]{:S(2)}) collective-permute-start(f32[144,128]{1,0:T(8,128)S(1)} %collective-permute-done.1.refs_1_), channel_id=1, source_target_pairs={{0,4},{1,5},{2,6},{3,7},{4,0},{5,1},{6,2},{7,3},{8,12},{9,13},{10,... | collective-permute-start | bytes 221192 | tf_op jit(solution)/shard_map/ppermute | solution.py:333

commit v6 on v4

--- a/solution.py
+++ b/solution.py
@@ -23,21 +23,21 @@
     (0, (
         ((3, 1, 0, 2), (3, 1, 0, 2)),
         ((2, 3, 1, 0), (2, 3, 1, 0)),
-        ((3, 1, 0, 2), (1, 3, 0, 2)),
-        ((0, 3, 2, 1), (2, 3, 1, 0)),
+        ((3, 0, 1, 2), (0, 3, 1, 2)),
+        ((0, 3, 2, 1), (3, 2, 1, 0)),
     )),
+    (1, 0),
     (1, (
         ((2, 0, 1, 3), (0, 2, 1, 3)),
         ((0, 1, 2, 3), (1, 0, 3, 2)),
-        ((0, 2, 3, 1), (2, 0, 3, 1)),
-        ((2, 1, 0, 3), (1, 0, 2, 3)),
+        ((1, 2, 3, 0), (2, 1, 3, 0)),
+        ((2, 1, 0, 3), (1, 0, 3, 2)),
     )),
-    (1, 0),
     (0, (
         ((2, 0, 1, 3), (2, 0, 1, 3)),
         ((1, 0, 2, 3), (1, 0, 2, 3)),
-        ((0, 2, 1, 3), (2, 0, 1, 3)),
-        ((1, 2, 3, 0), (0, 1, 3, 2)),
+        ((2, 1, 0, 3), (2, 1, 0, 3)),
+        ((2, 1, 3, 0), (1, 0, 3, 2)),
     )),
     (None, 1),
 )

time: 16.7 us -> 16.7 us (level)
  no operation moved by 1% of the time
where the time goes in v6:
time: 16.7 us; the launch traced here: 16.5 us
  starting transfers between devices  9 us (54%)
  waiting for transfers between devices  4.02 us (24%)
  Pallas kernels  3.47 us (21%)
    ppermute x6, starting transfers between devices, permute(): return lax.ppermute(value, ('pt', 'tm'), list(enumerate(targets)))  9 us
    ppermute x6, waiting for transfers between devices, permute(): return lax.ppermute(value, ('pt', 'tm'), list(enumerate(targets)))  4.02 us
    pallas_call x1, Pallas kernels, project(): pl.pallas_call(project_kernel, out_shape=jax.ShapeDtypeStruct(((pairs + 1...  2.26 us
    pallas_call x1, Pallas kernels, body(): pl.pallas_call(functools.partial(tiles_kernel, origins, chips, ratio, sca...  1.21 us
  transfers between devices with their start and end apart: 6, of which 4 were waited for; matrix products, arithmetic and copies ran while one was open for 0% of the time, Pallas kernels for 0%

profile of v6, /device:TPU:0, one launch (start us, length us, event | category | flops | bytes accessed | tf_op | source)
XLA Modules:
  0.0 16.5 jit_solution(6653503783721690410)
XLA Ops:
  0.0 2.3 %project.1 = f32[72,128]{1,0:T(8,128)S(1)} custom-call(s32[4]{0:T(128)} %bins_hbm.1, f32[64,8192]{1,0:T(8,128)} %signals_ref.1), custom_call_target="tpu_custom_call" | custom-call | tf_op jit(solution)/shard_map/project/pallas_call | solution.py:120
  2.3 0.5 %collective-permute-start = (f32[72,128]{1,0:T(8,128)S(1)}, f32[72,128]{1,0:T(8,128)S(1)}, u32[]{:S(2)}, u32[]{:S(2)}) collective-permute-start(f32[72,128]{1,0:T(8,128)S(1)} %project.1), channel_id=1, source_target_pairs={{0,1},{1,0},{2,3},{3,2},{4,5},{5,4},{6,7},{7,6},{8,9},{9,8},{10,11... | collective-permute-start | bytes 110600 | tf_op jit(solution)/shard_map/ppermute | solution.py:259
  2.8 0.9 %collective-permute-done = f32[72,128]{1,0:T(8,128)S(1)} collective-permute-done((f32[72,128]{1,0:T(8,128)S(1)}, f32[72,128]{1,0:T(8,128)S(1)}, u32[]{:S(2)}, u32[]{:S(2)}) %collective-permute-start) | collective-permute-done | bytes 36896 | tf_op jit(solution)/shard_map/ppermute | solution.py:259
  3.7 4.9 %collective-permute-start.4 = (f32[144,128]{1,0:T(8,128)S(1)}, f32[144,128]{1,0:T(8,128)S(1)}, u32[]{:S(2)}, u32[]{:S(2)}) collective-permute-start(f32[144,128]{1,0:T(8,128)S(1)} %pad_maximum_fusion.refs_0_), channel_id=1, source_target_pairs={{0,24},{1,8},{2,0},{3,16},{4,28},{5,12},{6,4},{7,20},{8,17},{9,25}... | collective-permute-start | bytes 221192 | tf_op jit(solution)/shard_map/ppermute | solution.py:259
  8.6 1.2 %collective-permute-start.3 = (f32[144,128]{1,0:T(8,128)S(1)}, f32[144,128]{1,0:T(8,128)S(1)}, u32[]{:S(2)}, u32[]{:S(2)}) collective-permute-start(f32[144,128]{1,0:T(8,128)S(1)} %pad_maximum_fusion.refs_0_), channel_id=1, source_target_pairs={{0,20},{1,4},{2,12},{3,28},{4,0},{5,16},{6,8},{7,24},{8,5},{9,13},... | collective-permute-start | bytes 221192 | tf_op jit(solution)/shard_map/ppermute | solution.py:259
  9.8 0.4 %collective-permute-start.2 = (f32[144,128]{1,0:T(8,128)S(1)}, f32[144,128]{1,0:T(8,128)S(1)}, u32[]{:S(2)}, u32[]{:S(2)}) collective-permute-start(f32[144,128]{1,0:T(8,128)S(1)} %pad_maximum_fusion.refs_0_), channel_id=1, source_target_pairs={{0,16},{1,0},{2,8},{3,24},{4,20},{5,4},{6,12},{7,28},{8,9},{9,1},{... | collective-permute-start | bytes 221192 | tf_op jit(solution)/shard_map/ppermute | solution.py:259
  10.2 0.5 %collective-permute-start.1 = (f32[144,128]{1,0:T(8,128)S(1)}, f32[144,128]{1,0:T(8,128)S(1)}, u32[]{:S(2)}, u32[]{:S(2)}) collective-permute-start(f32[144,128]{1,0:T(8,128)S(1)} %pad_maximum_fusion.refs_0_), channel_id=1, source_target_pairs={{0,2},{1,3},{2,0},{3,1},{4,6},{5,7},{6,4},{7,5},{8,10},{9,11},{10,... | collective-permute-start | bytes 221192 | tf_op jit(solution)/shard_map/ppermute | solution.py:259
  10.7 0.0 collective-permute-done.4.refs_5_
  10.7 1.4 %collective-permute-start.5 = (f32[144,128]{1,0:T(8,128)S(1)}, f32[144,128]{1,0:T(8,128)S(1)}, u32[]{:S(2)}, u32[]{:S(2)}) collective-permute-start(f32[144,128]{1,0:T(8,128)S(1)} %collective-permute-done.4.refs_5_), channel_id=1, source_target_pairs={{0,4},{1,5},{2,6},{3,7},{4,0},{5,1},{6,2},{7,3},{8,12},{9,13},{10,... | collective-permute-start | bytes 221192 | tf_op jit(solution)/shard_map/ppermute | solution.py:259
  12.1 1.0 %collective-permute-done.3.refs_3_ = f32[144,128]{1,0:T(8,128)S(1)} collective-permute-done((f32[144,128]{1,0:T(8,128)S(1)}, f32[144,128]{1,0:T(8,128)S(1)}, u32[]{:S(2)}, u32[]{:S(2)}) %collective-permute-start.3) | collective-permute-done | bytes 73760 | tf_op jit(solution)/shard_map/ppermute | solution.py:259
  13.2 0.0 collective-permute-done.2.refs_2_
  13.2 1.9 %collective-permute-done.1.refs_1_ = f32[144,128]{1,0:T(8,128)S(1)} collective-permute-done((f32[144,128]{1,0:T(8,128)S(1)}, f32[144,128]{1,0:T(8,128)S(1)}, u32[]{:S(2)}, u32[]{:S(2)}) %collective-permute-start.1) | collective-permute-done | bytes 73760 | tf_op jit(solution)/shard_map/ppermute | solution.py:259
  15.1 0.2 %collective-permute-done.5.refs_4_ = f32[144,128]{1,0:T(8,128)S(1)} collective-permute-done((f32[144,128]{1,0:T(8,128)S(1)}, f32[144,128]{1,0:T(8,128)S(1)}, u32[]{:S(2)}, u32[]{:S(2)}) %collective-permute-start.5) | collective-permute-done | bytes 73760 | tf_op jit(solution)/shard_map/ppermute | solution.py:259
  15.3 1.2 %tiles.1 = f32[2,4,64,128]{3,2,1,0:T(8,128)} custom-call(f32[144,128]{1,0:T(8,128)S(1)} %pad_maximum_fusion.refs_0_, f32[144,128]{1,0:T(8,128)S(1)} %collective-permute-done.1.refs_1_, f32[144,128]{1,0:T(8,128)S(1)} %collective-permute-done.2.refs_2_, f32[144,128]{1,0:T(8,128)S(1)} %collective-permute-done.3.refs_3_, ...), custom_call_target="tpu_custom_call" | custom-call | tf_op jit(solution)/shard_map/tiles/pallas_call | solution.py:283
  (1 shorter events, 0.0 us)
Async XLA Ops:
  2.3 1.4 %collective-permute-start = (f32[72,128]{1,0:T(8,128)S(1)}, f32[72,128]{1,0:T(8,128)S(1)}, u32[]{:S(2)}, u32[]{:S(2)}) collective-permute-start(f32[72,128]{1,0:T(8,128)S(1)} %project.1), channel_id=1, source_target_pairs={{0,1},{1,0},{2,3},{3,2},{4,5},{5,4},{6,7},{7,6},{8,9},{9,8},{10,11... | collective-permute-start | bytes 110600 | tf_op jit(solution)/shard_map/ppermute | solution.py:259
  3.7 7.1 %collective-permute-start.4 = (f32[144,128]{1,0:T(8,128)S(1)}, f32[144,128]{1,0:T(8,128)S(1)}, u32[]{:S(2)}, u32[]{:S(2)}) collective-permute-start(f32[144,128]{1,0:T(8,128)S(1)} %pad_maximum_fusion.refs_0_), channel_id=1, source_target_pairs={{0,24},{1,8},{2,0},{3,16},{4,28},{5,12},{6,4},{7,20},{8,17},{9,25}... | collective-permute-start | bytes 221192 | tf_op jit(solution)/shard_map/ppermute | solution.py:259
  8.6 4.6 %collective-permute-start.3 = (f32[144,128]{1,0:T(8,128)S(1)}, f32[144,128]{1,0:T(8,128)S(1)}, u32[]{:S(2)}, u32[]{:S(2)}) collective-permute-start(f32[144,128]{1,0:T(8,128)S(1)} %pad_maximum_fusion.refs_0_), channel_id=1, source_target_pairs={{0,20},{1,4},{2,12},{3,28},{4,0},{5,16},{6,8},{7,24},{8,5},{9,13},... | collective-permute-start | bytes 221192 | tf_op jit(solution)/shard_map/ppermute | solution.py:259
  9.8 3.3 %collective-permute-start.2 = (f32[144,128]{1,0:T(8,128)S(1)}, f32[144,128]{1,0:T(8,128)S(1)}, u32[]{:S(2)}, u32[]{:S(2)}) collective-permute-start(f32[144,128]{1,0:T(8,128)S(1)} %pad_maximum_fusion.refs_0_), channel_id=1, source_target_pairs={{0,16},{1,0},{2,8},{3,24},{4,20},{5,4},{6,12},{7,28},{8,9},{9,1},{... | collective-permute-start | bytes 221192 | tf_op jit(solution)/shard_map/ppermute | solution.py:259
  10.2 4.8 %collective-permute-start.1 = (f32[144,128]{1,0:T(8,128)S(1)}, f32[144,128]{1,0:T(8,128)S(1)}, u32[]{:S(2)}, u32[]{:S(2)}) collective-permute-start(f32[144,128]{1,0:T(8,128)S(1)} %pad_maximum_fusion.refs_0_), channel_id=1, source_target_pairs={{0,2},{1,3},{2,0},{3,1},{4,6},{5,7},{6,4},{7,5},{8,10},{9,11},{10,... | collective-permute-start | bytes 221192 | tf_op jit(solution)/shard_map/ppermute | solution.py:259
  10.7 4.6 %collective-permute-start.5 = (f32[144,128]{1,0:T(8,128)S(1)}, f32[144,128]{1,0:T(8,128)S(1)}, u32[]{:S(2)}, u32[]{:S(2)}) collective-permute-start(f32[144,128]{1,0:T(8,128)S(1)} %collective-permute-done.4.refs_5_), channel_id=1, source_target_pairs={{0,4},{1,5},{2,6},{3,7},{4,0},{5,1},{6,2},{7,3},{8,12},{9,13},{10,... | collective-permute-start | bytes 221192 | tf_op jit(solution)/shard_map/ppermute | solution.py:259

commit v7 on v6

--- a/solution.py
+++ b/solution.py
@@ -206,7 +206,10 @@
         dot = functools.partial(
             lax.dot_general, dimension_numbers=CONTRACT_FIRST, preferred_element_type=jnp.float32
         )
-        tile = dot(lhs_high, rhs_high) + (dot(lhs_high, rhs_low) + dot(lhs_low, rhs_high))
+        tile = dot(
+            jnp.concatenate([lhs_high, lhs_high, lhs_low], axis=0),
+            jnp.concatenate([rhs_high, rhs_low, rhs_high], axis=0),
+        )
         tile = tile * scale
         out_ref[0, f] = tile[:points]
         out_ref[1, f] = tile[points:]

time: 16.7 us -> 16.7 us (level)
  no operation moved by 1% of the time
where the time goes in v7:
time: 16.7 us; the launch traced here: 16.5 us
  starting transfers between devices  9 us (54%)
  waiting for transfers between devices  4.02 us (24%)
  Pallas kernels  3.47 us (21%)
    ppermute x6, starting transfers between devices, permute(): return lax.ppermute(value, ('pt', 'tm'), list(enumerate(targets)))  9 us
    ppermute x6, waiting for transfers between devices, permute(): return lax.ppermute(value, ('pt', 'tm'), list(enumerate(targets)))  4.02 us
    pallas_call x1, Pallas kernels, project(): pl.pallas_call(project_kernel, out_shape=jax.ShapeDtypeStruct(((pairs + 1...  2.26 us
    pallas_call x1, Pallas kernels, body(): pl.pallas_call(functools.partial(tiles_kernel, origins, chips, ratio, sca...  1.22 us
  transfers between devices with their start and end apart: 6, of which 4 were waited for; matrix products, arithmetic and copies ran while one was open for 0% of the time, Pallas kernels for 0%

profile of v7, /device:TPU:0, one launch (start us, length us, event | category | flops | bytes accessed | tf_op | source)
XLA Modules:
  0.0 16.5 jit_solution(768032913116056877)
XLA Ops:
  0.0 2.3 %project.1 = f32[72,128]{1,0:T(8,128)S(1)} custom-call(s32[4]{0:T(128)} %bins_hbm.1, f32[64,8192]{1,0:T(8,128)} %signals_ref.1), custom_call_target="tpu_custom_call" | custom-call | tf_op jit(solution)/shard_map/project/pallas_call | solution.py:120
  2.3 0.5 %collective-permute-start = (f32[72,128]{1,0:T(8,128)S(1)}, f32[72,128]{1,0:T(8,128)S(1)}, u32[]{:S(2)}, u32[]{:S(2)}) collective-permute-start(f32[72,128]{1,0:T(8,128)S(1)} %project.1), channel_id=1, source_target_pairs={{0,1},{1,0},{2,3},{3,2},{4,5},{5,4},{6,7},{7,6},{8,9},{9,8},{10,11... | collective-permute-start | bytes 110600 | tf_op jit(solution)/shard_map/ppermute | solution.py:262
  2.8 0.9 %collective-permute-done = f32[72,128]{1,0:T(8,128)S(1)} collective-permute-done((f32[72,128]{1,0:T(8,128)S(1)}, f32[72,128]{1,0:T(8,128)S(1)}, u32[]{:S(2)}, u32[]{:S(2)}) %collective-permute-start) | collective-permute-done | bytes 36896 | tf_op jit(solution)/shard_map/ppermute | solution.py:262
  3.7 4.9 %collective-permute-start.4 = (f32[144,128]{1,0:T(8,128)S(1)}, f32[144,128]{1,0:T(8,128)S(1)}, u32[]{:S(2)}, u32[]{:S(2)}) collective-permute-start(f32[144,128]{1,0:T(8,128)S(1)} %pad_maximum_fusion.refs_0_), channel_id=1, source_target_pairs={{0,24},{1,8},{2,0},{3,16},{4,28},{5,12},{6,4},{7,20},{8,17},{9,25}... | collective-permute-start | bytes 221192 | tf_op jit(solution)/shard_map/ppermute | solution.py:262
  8.6 1.2 %collective-permute-start.3 = (f32[144,128]{1,0:T(8,128)S(1)}, f32[144,128]{1,0:T(8,128)S(1)}, u32[]{:S(2)}, u32[]{:S(2)}) collective-permute-start(f32[144,128]{1,0:T(8,128)S(1)} %pad_maximum_fusion.refs_0_), channel_id=1, source_target_pairs={{0,20},{1,4},{2,12},{3,28},{4,0},{5,16},{6,8},{7,24},{8,5},{9,13},... | collective-permute-start | bytes 221192 | tf_op jit(solution)/shard_map/ppermute | solution.py:262
  9.8 0.4 %collective-permute-start.2 = (f32[144,128]{1,0:T(8,128)S(1)}, f32[144,128]{1,0:T(8,128)S(1)}, u32[]{:S(2)}, u32[]{:S(2)}) collective-permute-start(f32[144,128]{1,0:T(8,128)S(1)} %pad_maximum_fusion.refs_0_), channel_id=1, source_target_pairs={{0,16},{1,0},{2,8},{3,24},{4,20},{5,4},{6,12},{7,28},{8,9},{9,1},{... | collective-permute-start | bytes 221192 | tf_op jit(solution)/shard_map/ppermute | solution.py:262
  10.2 0.5 %collective-permute-start.1 = (f32[144,128]{1,0:T(8,128)S(1)}, f32[144,128]{1,0:T(8,128)S(1)}, u32[]{:S(2)}, u32[]{:S(2)}) collective-permute-start(f32[144,128]{1,0:T(8,128)S(1)} %pad_maximum_fusion.refs_0_), channel_id=1, source_target_pairs={{0,2},{1,3},{2,0},{3,1},{4,6},{5,7},{6,4},{7,5},{8,10},{9,11},{10,... | collective-permute-start | bytes 221192 | tf_op jit(solution)/shard_map/ppermute | solution.py:262
  10.7 0.0 collective-permute-done.4.refs_5_
  10.7 1.4 %collective-permute-start.5 = (f32[144,128]{1,0:T(8,128)S(1)}, f32[144,128]{1,0:T(8,128)S(1)}, u32[]{:S(2)}, u32[]{:S(2)}) collective-permute-start(f32[144,128]{1,0:T(8,128)S(1)} %collective-permute-done.4.refs_5_), channel_id=1, source_target_pairs={{0,4},{1,5},{2,6},{3,7},{4,0},{5,1},{6,2},{7,3},{8,12},{9,13},{10,... | collective-permute-start | bytes 221192 | tf_op jit(solution)/shard_map/ppermute | solution.py:262
  12.1 1.0 %collective-permute-done.3.refs_3_ = f32[144,128]{1,0:T(8,128)S(1)} collective-permute-done((f32[144,128]{1,0:T(8,128)S(1)}, f32[144,128]{1,0:T(8,128)S(1)}, u32[]{:S(2)}, u32[]{:S(2)}) %collective-permute-start.3) | collective-permute-done | bytes 73760 | tf_op jit(solution)/shard_map/ppermute | solution.py:262
  13.2 0.0 collective-permute-done.2.refs_2_
  13.2 1.9 %collective-permute-done.1.refs_1_ = f32[144,128]{1,0:T(8,128)S(1)} collective-permute-done((f32[144,128]{1,0:T(8,128)S(1)}, f32[144,128]{1,0:T(8,128)S(1)}, u32[]{:S(2)}, u32[]{:S(2)}) %collective-permute-start.1) | collective-permute-done | bytes 73760 | tf_op jit(solution)/shard_map/ppermute | solution.py:262
  15.1 0.2 %collective-permute-done.5.refs_4_ = f32[144,128]{1,0:T(8,128)S(1)} collective-permute-done((f32[144,128]{1,0:T(8,128)S(1)}, f32[144,128]{1,0:T(8,128)S(1)}, u32[]{:S(2)}, u32[]{:S(2)}) %collective-permute-start.5) | collective-permute-done | bytes 73760 | tf_op jit(solution)/shard_map/ppermute | solution.py:262
  15.3 1.2 %tiles.1 = f32[2,4,64,128]{3,2,1,0:T(8,128)} custom-call(f32[144,128]{1,0:T(8,128)S(1)} %pad_maximum_fusion.refs_0_, f32[144,128]{1,0:T(8,128)S(1)} %collective-permute-done.1.refs_1_, f32[144,128]{1,0:T(8,128)S(1)} %collective-permute-done.2.refs_2_, f32[144,128]{1,0:T(8,128)S(1)} %collective-permute-done.3.refs_3_, ...), custom_call_target="tpu_custom_call" | custom-call | tf_op jit(solution)/shard_map/tiles/pallas_call | solution.py:286
  (1 shorter events, 0.0 us)
Async XLA Ops:
  2.3 1.4 %collective-permute-start = (f32[72,128]{1,0:T(8,128)S(1)}, f32[72,128]{1,0:T(8,128)S(1)}, u32[]{:S(2)}, u32[]{:S(2)}) collective-permute-start(f32[72,128]{1,0:T(8,128)S(1)} %project.1), channel_id=1, source_target_pairs={{0,1},{1,0},{2,3},{3,2},{4,5},{5,4},{6,7},{7,6},{8,9},{9,8},{10,11... | collective-permute-start | bytes 110600 | tf_op jit(solution)/shard_map/ppermute | solution.py:262
  3.7 7.1 %collective-permute-start.4 = (f32[144,128]{1,0:T(8,128)S(1)}, f32[144,128]{1,0:T(8,128)S(1)}, u32[]{:S(2)}, u32[]{:S(2)}) collective-permute-start(f32[144,128]{1,0:T(8,128)S(1)} %pad_maximum_fusion.refs_0_), channel_id=1, source_target_pairs={{0,24},{1,8},{2,0},{3,16},{4,28},{5,12},{6,4},{7,20},{8,17},{9,25}... | collective-permute-start | bytes 221192 | tf_op jit(solution)/shard_map/ppermute | solution.py:262
  8.6 4.6 %collective-permute-start.3 = (f32[144,128]{1,0:T(8,128)S(1)}, f32[144,128]{1,0:T(8,128)S(1)}, u32[]{:S(2)}, u32[]{:S(2)}) collective-permute-start(f32[144,128]{1,0:T(8,128)S(1)} %pad_maximum_fusion.refs_0_), channel_id=1, source_target_pairs={{0,20},{1,4},{2,12},{3,28},{4,0},{5,16},{6,8},{7,24},{8,5},{9,13},... | collective-permute-start | bytes 221192 | tf_op jit(solution)/shard_map/ppermute | solution.py:262
  9.8 3.3 %collective-permute-start.2 = (f32[144,128]{1,0:T(8,128)S(1)}, f32[144,128]{1,0:T(8,128)S(1)}, u32[]{:S(2)}, u32[]{:S(2)}) collective-permute-start(f32[144,128]{1,0:T(8,128)S(1)} %pad_maximum_fusion.refs_0_), channel_id=1, source_target_pairs={{0,16},{1,0},{2,8},{3,24},{4,20},{5,4},{6,12},{7,28},{8,9},{9,1},{... | collective-permute-start | bytes 221192 | tf_op jit(solution)/shard_map/ppermute | solution.py:262
  10.2 4.8 %collective-permute-start.1 = (f32[144,128]{1,0:T(8,128)S(1)}, f32[144,128]{1,0:T(8,128)S(1)}, u32[]{:S(2)}, u32[]{:S(2)}) collective-permute-start(f32[144,128]{1,0:T(8,128)S(1)} %pad_maximum_fusion.refs_0_), channel_id=1, source_target_pairs={{0,2},{1,3},{2,0},{3,1},{4,6},{5,7},{6,4},{7,5},{8,10},{9,11},{10,... | collective-permute-start | bytes 221192 | tf_op jit(solution)/shard_map/ppermute | solution.py:262
  10.7 4.6 %collective-permute-start.5 = (f32[144,128]{1,0:T(8,128)S(1)}, f32[144,128]{1,0:T(8,128)S(1)}, u32[]{:S(2)}, u32[]{:S(2)}) collective-permute-start(f32[144,128]{1,0:T(8,128)S(1)} %collective-permute-done.4.refs_5_), channel_id=1, source_target_pairs={{0,4},{1,5},{2,6},{3,7},{4,0},{5,1},{6,2},{7,3},{8,12},{9,13},{10,... | collective-permute-start | bytes 221192 | tf_op jit(solution)/shard_map/ppermute | solution.py:262
